TPU v7x, 256 devices: a whole 4x4x8 slice. The times are simulated.
256 devices in a mesh: frame: 8 (over x, core), pixel: 32 (over y, z).
Axes of the slice: x: 4, y: 4, z: 8, core: 2. Of those that a mesh axis runs over, the one named last changes fastest.
Arguments:
- frames: bfloat16 [1024, 131072], P('frame', 'pixel'), may hold values from -6 to 6
- dead_time: float32 [131072], P('pixel'), may hold values from 0.002 to 0.02
- band_width: int32 [131072], P('pixel'), may hold values from 0 to 8
- cycle_label: int32 [131072], P('pixel'), may hold values from 0 to 1, as said below
- valid: int32 [131072], P('pixel'), may hold values from 0 to 1
Outputs:
- two_time: float32 [1024, 2, 1024], P(('frame', 'pixel'))
Inputs may be any that keep to these rules, and one draw needn't show every extreme that they name: `cycle_label`: every cycle holds at least one pixel with valid 1.
All inputs are finite; a program needn't handle non-finite values.
Results may differ from a plain program's by a relative error of at most 0.004.
Values may be sent and summed in bfloat16 or wider, within the bound.
A program may use at most 64 MiB of HBM per device.

v0:
```python
import jax
import jax.numpy as jnp
from jax import lax
from jax.sharding import PartitionSpec as P

CYCLES = 2
BAND = 8


def band_smooth(running, width_local, nframes):
    npixels = running.shape[1]
    frame_idx = jnp.arange(nframes, dtype=jnp.int32)[:, None]
    total = jnp.zeros((nframes, npixels), jnp.float32)
    divisor = jnp.ones((nframes, npixels), jnp.float32)
    for width in range(BAND + 1):
        if width > 0:
            upper_rows = jnp.concatenate(
                [
                    running[width + 1 :],
                    jnp.broadcast_to(running[nframes : nframes + 1], (width, npixels)),
                ],
                axis=0,
            )
            lower_rows = jnp.concatenate(
                [jnp.broadcast_to(running[0:1], (width, npixels)), running[0 : nframes - width]],
                axis=0,
            )
        else:
            upper_rows = running[1:]
            lower_rows = running[0:nframes]
        span = (
            jnp.minimum(frame_idx + width, nframes - 1) - jnp.maximum(frame_idx - width, 0) + 1
        ).astype(jnp.float32)
        chosen = width_local[None, :] == width
        total = jnp.where(chosen, upper_rows - lower_rows, total)
        divisor = jnp.where(chosen, span, divisor)
    return (total / divisor).astype(jnp.bfloat16)


def shards(frames, dead_time, band_width, cycle_label, valid):
    local = lax.all_to_all(frames, "frame", split_axis=1, concat_axis=0, tiled=True)
    nframes = local.shape[0]
    npixels = local.shape[1]
    offset = lax.axis_index("frame") * npixels
    dead_local = lax.dynamic_slice_in_dim(dead_time, offset, npixels, 0)
    width_local = lax.dynamic_slice_in_dim(band_width, offset, npixels, 0)
    label_local = lax.dynamic_slice_in_dim(cycle_label, offset, npixels, 0)
    valid_local = lax.dynamic_slice_in_dim(valid, offset, npixels, 0)
    count_rate = 4.0 + local.astype(jnp.float32)
    corrected = count_rate / (1.0 - dead_local[None, :] * count_rate)
    running = jnp.concatenate(
        [jnp.zeros((1, npixels), jnp.float32), jnp.cumsum(corrected, axis=0)], axis=0
    )
    smoothed = band_smooth(running, width_local, nframes)
    cycle_ids = jnp.arange(CYCLES, dtype=jnp.int32)[:, None]
    member = ((label_local[None, :] == cycle_ids) & (valid_local[None, :] == 1)).astype(
        jnp.bfloat16
    )
    counts = jnp.sum(member.astype(jnp.float32), axis=1)
    cycle_sum = lax.dot_general(
        smoothed, member, (((1,), (1,)), ((), ())), preferred_element_type=jnp.float32
    )
    cycle_sum, counts = lax.psum((cycle_sum, counts), ("frame", "pixel"))
    own_rows = nframes // lax.axis_size(("frame", "pixel"))
    weighted = (smoothed[:, None, :] * member[None, :, :]).reshape(
        lax.axis_size(("frame", "pixel")) * own_rows * CYCLES, npixels
    )
    product = lax.dot_general(
        weighted, smoothed, (((1,), (1,)), ((), ())), preferred_element_type=jnp.float32
    )
    gram = lax.psum_scatter(
        product.reshape(lax.axis_size(("frame", "pixel")) * own_rows, CYCLES * nframes),
        ("frame", "pixel"),
        scatter_dimension=0,
        tiled=True,
    )
    mean = cycle_sum / counts[None, :]
    row_start = (
        lax.axis_index("frame") * lax.axis_size("pixel") + lax.axis_index("pixel")
    ) * own_rows
    mean_rows = lax.dynamic_slice_in_dim(mean, row_start, own_rows, 0)
    gram = gram.reshape(own_rows, CYCLES, nframes)
    return gram / counts[None, :, None] - mean_rows[:, :, None] * jnp.transpose(mean)[None, :, :]


def solution(mesh):
    in_specs = (P("frame", "pixel"), P("pixel"), P("pixel"), P("pixel"), P("pixel"))
    out_specs = P(("frame", "pixel"), None, None)
    return jax.shard_map(shards, mesh=mesh, in_specs=in_specs, out_specs=out_specs, check_vma=False)
```

profile of v0, /device:TPU:1, one launch (start us, length us, event | category | flops | bytes accessed | tf_op | source)
XLA Modules:
  0.0 367.9 jit_solution(6129447735267489428)
XLA Ops:
  6.5 2.3 copy.20
  8.8 6.7 %all-to-all-start = ((bf16[128,8,512]{0,2,1:T(8,128)(2,1)}), bf16[128,8,512]{0,2,1:T(8,128)(2,1)S(1)}, u32[]{:S(2)}, u32[]{:S(2)}) async-start(bf16[128,8,512]{0,2,1:T(8,128)(2,1)} %bitcast), calls=%async_computation | async-start | bytes 2097152 | tf_op jit(solution)/shard_map/all_to_all | solution.py:41
  15.5 0.0 all-reduce.13.cloned.1.call-start
  15.5 0.8 dynamic_slice.16
  16.3 0.8 dynamic_slice.17
  17.0 0.8 broadcast_compare_fusion.8
  17.9 0.1 convert_reduce_fusion
  18.0 12.6 %all-to-all-done = bf16[128,8,512]{0,2,1:T(8,128)(2,1)S(1)} async-done(((bf16[128,8,512]{0,2,1:T(8,128)(2,1)}), bf16[128,8,512]{0,2,1:T(8,128)(2,1)S(1)}, u32[]{:S(2)}, u32[]{:S(2)}) %all-to-all-start) | async-done | bytes 1048608 | tf_op jit(solution)/shard_map/all_to_all | solution.py:41
  30.6 1.5 add_bitcast_fusion
  32.1 1.9 copy.21
  34.0 0.3 bitcast_divide_fusion
  34.3 1.3 fusion.10
  35.7 0.2 broadcast_add_fusion
  35.9 1.2 copy.23
  37.2 0.5 fusion.62
  37.7 0.7 fusion.63
  38.4 0.7 fusion.64
  39.1 0.7 fusion.65
  39.8 0.7 fusion.66
  40.5 0.7 fusion.67
  41.2 0.7 fusion.68
  41.9 1.8 fusion.61
  43.8 15.8 %fusion.12 = bf16[1024,512]{1,0:T(8,128)(2,1)S(1)} fusion(f32[1024,512]{1,0:T(8,128)S(1)} %bitcast.33, f32[1023,512]{1,0:T(8,128)S(1)} %get-tuple-element.24, f32[1,512]{1,0:T(1,128)S(1)} %slice.90, f32[1023,512]{1,0:T(8,128)S(1)} %get-tuple-element.23, f32[1022,512]{1,0:T(8,128)S(1)} %get-tuple-element.22, f32[2,512]{1,0:T(2,128)S(1)} %broadcast_in_dim.201, ...), kind=kLoop, calls=%fused_computation.23 | loop fusion | flops 19398656 | bytes 36667904 | tf_op jit(solution)/shard_map/convert_element_type | solution.py:37
  59.6 2.2 broadcast_multiply_fusion
  61.7 2.2 mul.53
  64.0 7.2 %fusion.69 = f32[2048,1024]{1,0:T(8,128)} fusion(bf16[2048,512]{1,0:T(8,128)(2,1)} %mul.53, bf16[1024,512]{1,0:T(8,128)(2,1)S(1)} %fusion.12), kind=kOutput, calls=%fused_computation.124 | convolution fusion | flops 2147483648 | bytes 11534336 | tf_op jit(solution)/shard_map/dot_general | solution.py:68
  71.2 9.9 %reshape.258 = f32[1024,2048]{1,0:T(8,128)} reshape(f32[2048,1024]{1,0:T(8,128)} %fusion.69) | data formatting | bytes 16777216 | tf_op jit(solution)/shard_map/reshape | solution.py:72
  81.1 0.0 all-reduce.13.cloned.1.call-update
  81.1 0.4 fusion.56
  81.5 78.4 %all-reduce.10 = (f32[2]{0:T(128)S(1)}, f32[1024,2]{0,1:T(2,128)S(1)}) all-reduce(f32[2]{0:T(128)S(1)} %get-tuple-element.7, f32[1024,2]{0,1:T(2,128)S(1)} %fusion.56), channel_id=1, replica_groups=mesh['frame'=8,'pixel'=32] {'frame','pixel'}, use_global_device_ids=true, to_apply=%region_4.5 | all-reduce | flops 2050 | bytes 16400 | tf_op jit(solution)/shard_map/psum | solution.py:63
  159.9 0.1 broadcast_divide_fusion
  159.9 0.1 constant_dynamic-slice_fusion.1
  160.0 0.1 copy.24
  160.1 0.1 fusion.73
  160.2 199.3 %all-reduce.13.cloned.1.call-done = f32[1024,2048]{1,0:T(8,128)} async-done(((f32[1024,2048]{1,0:T(8,128)}), f32[1024,2048]{1,0:T(8,128)}) %all-reduce.13.cloned.1.call-update) | async-done | bytes 8388624
  359.5 0.8 constant_dynamic-slice_fusion
  360.4 0.7 divide_subtract_fusion
  (17 shorter events, 0.1 us)
Async XLA Ops:
  8.8 21.8 %all-to-all-start = ((bf16[128,8,512]{0,2,1:T(8,128)(2,1)}), bf16[128,8,512]{0,2,1:T(8,128)(2,1)S(1)}, u32[]{:S(2)}, u32[]{:S(2)}) async-start(bf16[128,8,512]{0,2,1:T(8,128)(2,1)} %bitcast), calls=%async_computation | async-start | bytes 2097152 | tf_op jit(solution)/shard_map/all_to_all | solution.py:41
  15.5 344.0 %all-reduce.13.cloned.1.call-start = ((), (), s32[]{:S(2)}) async-start(), calls=%async_computation.1 | async-start | bytes 16777216
Sparse Core Ops, SparseCore 0:
  81.2 278.1 all-reduce.12
where the time goes:
time: 369 us; the launch traced here: 368 us
  waiting for transfers between devices  212 us (57%)
  blocking collectives  78.4 us (21%)
  local copies, waits for them, and re-layouts  26.7 us (7%)
  other arithmetic  23.1 us (6%)
  between operations  13.6 us (4%)
  matrix products  7.56 us (2%)
  starting transfers between devices  6.7 us (2%)
    unnamed x2, waiting for transfers between devices  199 us
    psum x1, blocking collectives, shards(): cycle_sum, counts = lax.psum((cycle_sum, counts), ('frame', 'pixel'))  78.4 us
    convert_element_type x1, other arithmetic, band_smooth(): return (total / divisor).astype(jnp.bfloat16)  15.8 us
    all_to_all x1, waiting for transfers between devices, shards(): lax.all_to_all(frames, 'frame', split_axis=1, concat_axis=0, tiled=True)  12.6 us
    reshape x1, local copies, waits for them, and re-layouts, shards(): product.reshape(lax.axis_size(('frame', 'pixel')) * own_rows, CYCLES * nf...  9.91 us
  transfers between devices with their start and end apart: 2, of which 2 were waited for; matrix products, arithmetic and copies ran while one was open for 1% of the time, Pallas kernels for 0%

commit v1 on v0

v1 whole, which is shorter than its diff:
```python
import functools

import jax
import jax.numpy as jnp
from jax import lax
from jax.experimental import pallas as pl
from jax.experimental.pallas import tpu as pltpu
from jax.sharding import PartitionSpec as P

MESH = pl.DeviceIdType.MESH
CYCLES = 2
BAND = 8
CORES = 2
NX = 4
NY = 4
NZ = 8
LANES = 128
GROUP = 32
NFRAMES = 1024
NDEV_FRAME = NX * CORES
OWN_FRAMES = NFRAMES // NDEV_FRAME
NPIX_GROUP = 4096
OWN_PIX = NPIX_GROUP // NDEV_FRAME
CHUNKS = OWN_PIX // LANES
CHIP_PIX = CORES * OWN_PIX
CLASS_ROWS = NFRAMES // 4
SUB_ROWS = CLASS_ROWS // 4
PAD = BAND
TILE = 256


def remote(src, dst, send_sem, recv_sem, device):
    return pltpu.make_async_remote_copy(
        src_ref=src,
        dst_ref=dst,
        send_sem=send_sem,
        recv_sem=recv_sem,
        device_id=device,
        device_id_type=MESH,
    )


def kernel(
    frames, dead_hbm, band_hbm, label_hbm, valid_hbm,
    out,
    dead, band, label, valid, arrived, rate, smooth, outgoing,
    lhs, gsend, grecv, gown, hsend, hrecv, hown, tsend, trecv,
    stat1, stat2, stat3, statg2, statg3, spread, spread_t,
    fsend, frecv,
    par_sem, own_sem, a2a_send, a2a_recv, sib_send, sib_recv,
    s1_send, s1_recv, s2_send, s2_recv, s3_send, s3_recv,
    g_send, g_recv, h_send, h_recv, t_send, t_recv, f_send, f_recv,
):
    f = lax.axis_index("frame")
    p = lax.axis_index("pixel")
    x, c = f // CORES, f % CORES
    y, z = p // NZ, p % NZ
    a1 = c * x + (1 - c) * y
    a2 = c * y + (1 - c) * x

    def first_peer(a):
        return ((c * a + (1 - c) * x) * CORES + c, (c * y + (1 - c) * a) * NZ + z)

    def second_peer(a):
        return ((c * x + (1 - c) * a) * CORES + c, (c * a + (1 - c) * y) * NZ + z)

    def z_peer(other):
        return (f, y * NZ + other)

    def frame_peer(other):
        return (other, p)

    sibling = (x * CORES + (1 - c), p)

    barrier = pltpu.get_barrier_semaphore()
    for k in range(1, NDEV_FRAME):
        pl.semaphore_signal(barrier, inc=1, device_id=frame_peer((f + k) % NDEV_FRAME), device_id_type=MESH)
    for k in range(1, NY):
        pl.semaphore_signal(barrier, inc=1, device_id=(f, ((y + k) % NY) * NZ + z), device_id_type=MESH)
    for k in range(1, NZ):
        pl.semaphore_signal(barrier, inc=1, device_id=z_peer((z + k) % NZ), device_id_type=MESH)
    pl.semaphore_wait(barrier, NDEV_FRAME - 1 + NY - 1 + NZ - 1)

    def piece(owner, chunk):
        return frames.at[:, pl.ds(pl.multiple_of(owner * OWN_PIX + chunk * LANES, LANES), LANES)]

    def a2a_copy(k, chunk):
        to = (f + k) % NDEV_FRAME
        return remote(
            piece(to, chunk), arrived.at[chunk, f], a2a_send.at[chunk, k], a2a_recv.at[chunk, f], frame_peer(to)
        )

    def own_copy(chunk):
        return pltpu.make_async_copy(piece(f, chunk), arrived.at[chunk, f], own_sem.at[chunk])

    for chunk in range(CHUNKS):
        for k in range(1, NDEV_FRAME):
            a2a_copy(k, chunk).start()
        own_copy(chunk).start()
    params = [
        pltpu.make_async_copy(src, dst, par_sem.at[n])
        for n, (src, dst) in enumerate(
            ((dead_hbm, dead), (band_hbm, band), (label_hbm, label), (valid_hbm, valid))
        )
    ]
    for copy in params:
        copy.start()
    rate[0:PAD, :] = jnp.zeros((PAD, LANES), jnp.float32)
    rate[PAD + NFRAMES : PAD + NFRAMES + PAD, :] = jnp.zeros((PAD, LANES), jnp.float32)
    for copy in params:
        copy.wait()

    def sib_copy(chunk):
        return remote(
            outgoing.at[chunk],
            smooth.at[:, pl.ds(OWN_PIX + chunk * LANES, LANES)],
            sib_send.at[chunk],
            sib_recv.at[chunk],
            sibling,
        )

    for chunk in range(CHUNKS):
        own_copy(chunk).wait()
        for k in range(1, NDEV_FRAME):
            source = (f + k) % NDEV_FRAME
            remote(
                piece(source, chunk), arrived.at[chunk, source], a2a_send.at[chunk, k],
                a2a_recv.at[chunk, source], frame_peer(source),
            ).wait_recv()
        row = f * CHUNKS + chunk
        dead_row = dead[pl.ds(row, 1), :]
        width = band[pl.ds(row, 1), :]
        cycle = label[pl.ds(row, 1), :]
        used = valid[pl.ds(row, 1), :] == 1
        mine = jnp.where(used & (cycle == c), 1.0, 0.0)
        other = jnp.where(used & (cycle == 1 - c), 1.0, 0.0)
        within = [jnp.where(width >= k, 1.0, 0.0) for k in range(1, BAND + 1)]
        full = 1.0 / (2 * width + 1).astype(jnp.float32)

        def correct(block, _):
            for half in range(OWN_FRAMES // GROUP):
                count = 4.0 + arrived[chunk, block, half * GROUP : (half + 1) * GROUP, :].astype(jnp.float32)
                rate[pl.ds(pl.multiple_of(PAD + block * OWN_FRAMES + half * GROUP, 8), GROUP), :] = count / (
                    1.0 - dead_row * count
                )
            return 0

        lax.fori_loop(0, NDEV_FRAME, correct, 0)

        def window(start):
            total = rate[pl.ds(start + PAD, GROUP), :]
            for k in range(1, BAND + 1):
                total = total + within[k - 1] * (
                    rate[pl.ds(start + PAD - k, GROUP), :] + rate[pl.ds(start + PAD + k, GROUP), :]
                )
            return total

        def put(start, value):
            rows = pl.ds(start, GROUP)
            smooth[rows, chunk * LANES : (chunk + 1) * LANES] = (value * mine).astype(jnp.bfloat16)
            outgoing[chunk, rows, :] = (value * other).astype(jnp.bfloat16)

        def inside(block, _):
            start = pl.multiple_of(block * GROUP, GROUP)
            put(start, window(start) * full)
            return 0

        for start in (0, NFRAMES - GROUP):
            frame = start + lax.broadcasted_iota(jnp.int32, (GROUP, LANES), 0)
            span = jnp.minimum(frame + width, NFRAMES - 1) - jnp.maximum(frame - width, 0) + 1
            put(start, window(start) / span.astype(jnp.float32))
        lax.fori_loop(1, NFRAMES // GROUP - 1, inside, 0)
        sib_copy(chunk).start()

    chip_label = label[pl.ds(pl.multiple_of(x * (CHIP_PIX // LANES), 8), CHIP_PIX // LANES), :]
    chip_valid = valid[pl.ds(pl.multiple_of(x * (CHIP_PIX // LANES), 8), CHIP_PIX // LANES), :]
    held = jnp.sum(jnp.where((chip_label == c) & (chip_valid == 1), 1.0, 0.0), axis=(0, 1), keepdims=True)

    for chunk in range(CHUNKS):
        sib_copy(chunk).wait_recv()

    contract_last = (((1,), (1,)), ((), ()))
    sums = lax.dot_general(
        jnp.ones((8, CHIP_PIX), jnp.bfloat16), smooth[...], contract_last, preferred_element_type=jnp.float32
    )[0:1, :]
    stat1[a1, 0:1, :] = sums
    stat1[a1, 1:2, :] = jnp.broadcast_to(held, (1, NFRAMES))

    def stat1_copy(k):
        to = (a1 + k) % 4
        return remote(stat1.at[a1], stat1.at[a1], s1_send.at[k], s1_recv.at[a1], first_peer(to))

    for k in range(1, 4):
        stat1_copy(k).start()

    def group_start(a, g):
        second, core = g // CORES, g % CORES
        row_x = c * a + (1 - c) * second
        row_y = c * second + (1 - c) * a
        return pl.multiple_of((row_x * 8 + core * 4 + row_y) * GROUP, GROUP)

    def g_copy(k, sub):
        to = (a1 + k) % 4
        rows = pl.ds(pl.multiple_of(sub * SUB_ROWS, SUB_ROWS), SUB_ROWS)
        return remote(
            gsend.at[to, rows, :], grecv.at[a1, rows, :], g_send.at[k, sub], g_recv.at[a1, sub], first_peer(to)
        )

    ones = jnp.ones((CHIP_PIX, LANES), jnp.bfloat16)
    for k in (1, 2, 3, 0):
        to = (a1 + k) % 4
        for g in range(8):
            lhs[g * GROUP : (g + 1) * GROUP, :] = smooth[pl.ds(group_start(to, g), GROUP), :]
        column = jnp.dot(lhs[...], ones, preferred_element_type=jnp.float32) / jnp.maximum(held, 1.0)

        def tile(n, _):
            cols = pl.ds(pl.multiple_of(n * TILE, TILE), TILE)
            product = lax.dot_general(
                lhs[...], smooth[cols, :], contract_last, preferred_element_type=jnp.float32
            )
            gown[:, cols] = product
            return 0

        lax.fori_loop(0, NFRAMES // TILE, tile, 0)
        for n in range(NFRAMES // LANES):
            cols = slice(n * LANES, (n + 1) * LANES)
            centred = gown[:, cols] - column * sums[:, cols]
            if k:
                gsend[to, :, cols] = centred.astype(jnp.bfloat16)
            else:
                gown[:, cols] = centred
        if k:
            for j in (1, 2, 3, 0):
                g_copy(k, (a2 + j) % 4).start()

    for k in range(1, 4):
        source = (a1 + k) % 4
        remote(stat1.at[source], stat1.at[source], s1_send.at[k], s1_recv.at[source], first_peer(source)).wait_recv()
    statg2[...] = stat1[0] + stat1[1] + stat1[2] + stat1[3]

    def stat2_copy(k):
        return remote(statg2, stat2.at[a2], s2_send.at[k], s2_recv.at[a2], second_peer((a2 + k) % 4))

    for k in range(1, 4):
        stat2_copy(k).start()
    total = statg2[...]
    for k in range(1, 4):
        source = (a2 + k) % 4
        remote(statg2, stat2.at[source], s2_send.at[k], s2_recv.at[source], second_peer(source)).wait_recv()
        total = total + stat2[source]
    statg3[...] = total

    def stat3_copy(k):
        return remote(statg3, stat3.at[z], s3_send.at[k], s3_recv.at[z], z_peer((z + k) % NZ))

    for k in range(1, NZ):
        stat3_copy(k).start()
    for k in range(1, NZ):
        source = (z + k) % NZ
        remote(statg3, stat3.at[source], s3_send.at[k], s3_recv.at[source], z_peer(source)).wait_recv()
        total = total + stat3[source]
    counts = total[1:2, :]
    mean = total[0:1, :] / counts

    spread[...] = jnp.zeros_like(spread)
    for k in range(4):
        spread[k : k + 1, :] = stat1[k, 0:1, :] / jnp.maximum(stat1[k, 1:2, :], 1.0) - mean
    spread_t[...] = jnp.transpose(spread[...])
    for k in range(4):
        spread[k : k + 1, :] = spread[k : k + 1, :] * stat1[k, 1:2, :]
    for g in range(8):
        rows = pl.ds(g * GROUP, GROUP)
        gown[rows, :] += jnp.dot(
            spread_t[pl.ds(group_start(a1, g), GROUP), :], spread[...],
            preferred_element_type=jnp.float32, precision=lax.Precision.HIGHEST,
        )

    def h_copy(k):
        to = (a2 + k) % 4
        return remote(hsend.at[to], hrecv.at[a2], h_send.at[k], h_recv.at[a2], second_peer(to))

    for j in (1, 2, 3, 0):
        sub = (a2 + j) % 4
        rows = pl.ds(pl.multiple_of(sub * SUB_ROWS, SUB_ROWS), SUB_ROWS)
        for k in range(1, 4):
            source = (a1 + k) % 4
            remote(
                gsend.at[source, rows, :], grecv.at[source, rows, :], g_send.at[k, sub], g_recv.at[source, sub],
                first_peer(source),
            ).wait_recv()
        value = gown[rows, :]
        for k in range(1, 4):
            value = value + grecv[(a1 + k) % 4, rows, :].astype(jnp.float32)
        if j:
            hsend[sub] = value.astype(jnp.bfloat16)
            h_copy(j).start()
        else:
            hown[...] = value

    for k in range(1, 4):
        source = (a2 + k) % 4
        remote(hsend.at[source], hrecv.at[source], h_send.at[k], h_recv.at[source], second_peer(source)).wait_recv()
    value = hown[...]
    for k in range(1, 4):
        value = value + hrecv[(a2 + k) % 4].astype(jnp.float32)
    hown[...] = value
    own_rows = GROUP // NZ

    for other_z in range(NZ):
        rows = jnp.concatenate(
            [hown[core * GROUP + other_z * own_rows : core * GROUP + (other_z + 1) * own_rows, :] for core in range(CORES)],
            axis=0,
        )
        tsend[other_z] = rows.astype(jnp.bfloat16)

    def t_copy(k):
        to = (z + k) % NZ
        return remote(tsend.at[to], trecv.at[z], t_send.at[k], t_recv.at[z], z_peer(to))

    for k in range(1, NZ):
        t_copy(k).start()
    value = tsend[z].astype(jnp.float32)
    for k in range(1, NZ):
        source = (z + k) % NZ
        remote(tsend.at[source], trecv.at[source], t_send.at[k], t_recv.at[source], z_peer(source)).wait_recv()
        value = value + trecv[source].astype(jnp.float32)
    value = value / counts

    low, high = value[0:own_rows, :], value[own_rows : 2 * own_rows, :]
    fsend[...] = jnp.where(c == 0, high, low)
    last = remote(fsend, frecv, f_send, f_recv, sibling)
    last.start()
    out[c] = jnp.where(c == 0, low, high)
    last.wait_recv()
    out[1 - c] = frecv[...]

    for chunk in range(CHUNKS):
        for k in range(1, NDEV_FRAME):
            a2a_copy(k, chunk).wait_send()
        sib_copy(chunk).wait_send()
    for k in range(1, 4):
        stat1_copy(k).wait_send()
        stat2_copy(k).wait_send()
        h_copy(k).wait_send()
        for sub in range(4):
            g_copy(k, sub).wait_send()
    for k in range(1, NZ):
        stat3_copy(k).wait_send()
        t_copy(k).wait_send()
    last.wait_send()


def shards(frames, dead_time, band_width, cycle_label, valid):
    rows = NPIX_GROUP // LANES
    flat = [a.reshape(rows, LANES) for a in (dead_time, band_width, cycle_label, valid)]
    own_rows = GROUP // NZ
    dma = pltpu.SemaphoreType.DMA
    f32, bf16 = jnp.float32, jnp.bfloat16
    any_space = pl.BlockSpec(memory_space=pl.ANY)
    vmem = pltpu.VMEM
    out = pl.pallas_call(
        kernel,
        out_shape=jax.ShapeDtypeStruct((CYCLES, own_rows, NFRAMES), f32),
        in_specs=[any_space] * 5,
        out_specs=pl.BlockSpec(memory_space=pltpu.VMEM),
        scratch_shapes=[
            vmem((rows, LANES), f32),
            vmem((rows, LANES), jnp.int32),
            vmem((rows, LANES), jnp.int32),
            vmem((rows, LANES), jnp.int32),
            vmem((CHUNKS, NDEV_FRAME, OWN_FRAMES, LANES), bf16),
            vmem((PAD + NFRAMES + PAD, LANES), f32),
            vmem((NFRAMES, CHIP_PIX), bf16),
            vmem((CHUNKS, NFRAMES, LANES), bf16),
            vmem((CLASS_ROWS, CHIP_PIX), bf16),
            vmem((4, CLASS_ROWS, NFRAMES), bf16),
            vmem((4, CLASS_ROWS, NFRAMES), bf16),
            vmem((CLASS_ROWS, NFRAMES), f32),
            vmem((4, SUB_ROWS, NFRAMES), bf16),
            vmem((4, SUB_ROWS, NFRAMES), bf16),
            vmem((SUB_ROWS, NFRAMES), f32),
            vmem((NZ, CORES * own_rows, NFRAMES), bf16),
            vmem((NZ, CORES * own_rows, NFRAMES), bf16),
            vmem((4, 2, NFRAMES), f32),
            vmem((4, 2, NFRAMES), f32),
            vmem((NZ, 2, NFRAMES), f32),
            vmem((2, NFRAMES), f32),
            vmem((2, NFRAMES), f32),
            vmem((8, NFRAMES), f32),
            vmem((NFRAMES, 8), f32),
            vmem((own_rows, NFRAMES), f32),
            vmem((own_rows, NFRAMES), f32),
            dma((4,)),
            dma((CHUNKS,)),
            dma((CHUNKS, NDEV_FRAME)), dma((CHUNKS, NDEV_FRAME)),
            dma((CHUNKS,)), dma((CHUNKS,)),
            dma((4,)), dma((4,)),
            dma((4,)), dma((4,)),
            dma((NZ,)), dma((NZ,)),
            dma((4, 4)), dma((4, 4)),
            dma((4,)), dma((4,)),
            dma((NZ,)), dma((NZ,)),
            dma, dma,
        ],
        compiler_params=pltpu.CompilerParams(
            collective_id=0, has_side_effects=True, vmem_limit_bytes=48 * 2**20
        ),
    )(frames, *flat)
    return jnp.transpose(out, (1, 0, 2))


def solution(mesh):
    in_specs = (P("frame", "pixel"), P("pixel"), P("pixel"), P("pixel"), P("pixel"))
    out_specs = P(("frame", "pixel"), None, None)
    return jax.shard_map(shards, mesh=mesh, in_specs=in_specs, out_specs=out_specs, check_vma=False)
```

time: 369 us -> 64.1 us (0.17)
  waiting for transfers between devices: 212 us -> 0 us
  blocking collectives: 78.4 us -> 0 us
  Pallas kernels: 0 us -> 58.9 us
  other arithmetic: 23.1 us -> 0 us
  local copies, waits for them, and re-layouts: 26.7 us -> 4.73 us
  between operations: 13.6 us -> 0.01 us
  matrix products: 7.56 us -> 0 us
  starting transfers between devices: 6.7 us -> 0 us
    unnamed x2 -> x0, waiting for transfers between devices: 199 us -> none
    psum x1 -> x0, blocking collectives: 78.4 us -> none  [shards(): cycle_sum, counts = lax.psum((cycle_sum, counts), ('frame', 'pixel'))]
    pallas_call x0 -> x1, Pallas kernels: none -> 58.9 us  [shards(): pl.pallas_call(kernel, out_shape=jax.ShapeDtypeStruct((CYCLES, own_rows,...]
    convert_element_type x6 -> x0, other arithmetic: 15.8 us -> none  [the longest x1 15.8 us: band_smooth(): return (total / divisor).astype(jnp.bfloat16)]
    all_to_all x1 -> x0, waiting for transfers between devices: 12.6 us -> none  [shards(): lax.all_to_all(frames, 'frame', split_axis=1, concat_axis=0, tiled=True)]
    reshape x2 -> x0, local copies, waits for them, and re-layouts: 9.95 us -> none  [the longest x1 9.91 us: shards(): product.reshape(lax.axis_size(('frame', 'pixel')) * own_rows, CYCLES * nf...]
    dot_general x2 -> x0, matrix products: 7.56 us -> none  [the longest x1 7.19 us: shards(): lax.dot_general(weighted, smoothed, (((1,), (1,)), ((), ())), preferred_e...]
    all_to_all x1 -> x0, starting transfers between devices: 6.7 us -> none  [shards(): lax.all_to_all(frames, 'frame', split_axis=1, concat_axis=0, tiled=True)]
  transfers between devices with their start and end apart: 2 -> 0, of which waited for: 2 -> 0; matrix products, arithmetic and copies ran while one was open for 1% -> 0% of each run, Pallas kernels for 0% -> 0%
where the time goes in v1:
time: 64.1 us; the launch traced here: 63.7 us
  Pallas kernels  58.9 us (92%)
  local copies, waits for them, and re-layouts  4.73 us (7%)
    pallas_call x1, Pallas kernels, shards(): pl.pallas_call(kernel, out_shape=jax.ShapeDtypeStruct((CYCLES, own_rows,...  58.9 us
    unnamed x10, local copies, waits for them, and re-layouts  4.09 us

profile of v1, /device:TPU:1, one launch (start us, length us, event | category | flops | bytes accessed | tf_op | source)
XLA Modules:
  0.0 63.7 jit_solution(14457723832109837161)
XLA Ops:
  0.0 0.0 copy-start
  0.0 1.2 %copy-done = bf16[128,4096]{1,0:T(8,128)(2,1)S(1)} copy-done((bf16[128,4096]{1,0:T(8,128)(2,1)S(1)}, bf16[128,4096]{1,0:T(8,128)(2,1)}, u32[]{:S(2)}) %copy-start) | copy-done | bytes 1048600
  1.2 0.0 copy-start.1
  1.2 0.7 %copy-done.1 = f32[4096]{0:T(1024)S(1)} copy-done((f32[4096]{0:T(1024)S(1)}, f32[4096]{0:T(1024)}, u32[]{:S(2)}) %copy-start.1) | copy-done | bytes 16408
  1.9 0.0 copy-start.2
  1.9 0.7 %copy-done.2 = s32[4096]{0:T(1024)S(1)} copy-done((s32[4096]{0:T(1024)S(1)}, s32[4096]{0:T(1024)}, u32[]{:S(2)}) %copy-start.2) | copy-done | bytes 16408
  2.7 0.0 copy-start.3
  2.7 0.7 %copy-done.3 = s32[4096]{0:T(1024)S(1)} copy-done((s32[4096]{0:T(1024)S(1)}, s32[4096]{0:T(1024)}, u32[]{:S(2)}) %copy-start.3) | copy-done | bytes 16408
  3.4 0.0 copy-start.4
  3.4 0.7 %copy-done.4 = s32[4096]{0:T(1024)S(1)} copy-done((s32[4096]{0:T(1024)S(1)}, s32[4096]{0:T(1024)}, u32[]{:S(2)}) %copy-start.4) | copy-done | bytes 16408
  4.1 58.9 %shard_map.55 = f32[2,4,1024]{2,1,0:T(4,128)S(1)} custom-call(bf16[128,4096]{1,0:T(8,128)(2,1)S(1)} %copy-done, f32[32,128]{1,0:T(8,128)S(1)} %bitcast.6, s32[32,128]{1,0:T(8,128)S(1)} %bitcast.7, s32[32,128]{1,0:T(8,128)S(1)} %bitcast.8, s32[32,128]{1,0:T(8,128)S(1)} %bitcast.9), custom_call_target="tpu_custom_call" | custom-call | tf_op jit(solution)/shard_map/pallas_call | solution.py:361
  63.0 0.6 %copy.6 = f32[4,2,1024]{2,1,0:T(2,128)} copy(f32[4,2,1024]{2,0,1:T(4,128)S(1)} %bitcast.5) | data formatting | bytes 65536 | tf_op jit(solution)/shard_map/transpose | solution.py:409
Async XLA Ops:
  0.0 1.2 %copy-start = (bf16[128,4096]{1,0:T(8,128)(2,1)S(1)}, bf16[128,4096]{1,0:T(8,128)(2,1)}, u32[]{:S(2)}) copy-start(bf16[128,4096]{1,0:T(8,128)(2,1)} %frames.1) | copy-start | bytes 3145732
  1.2 0.7 %copy-start.1 = (f32[4096]{0:T(1024)S(1)}, f32[4096]{0:T(1024)}, u32[]{:S(2)}) copy-start(f32[4096]{0:T(1024)} %param.6) | copy-start | bytes 49156
  1.9 0.7 %copy-start.2 = (s32[4096]{0:T(1024)S(1)}, s32[4096]{0:T(1024)}, u32[]{:S(2)}) copy-start(s32[4096]{0:T(1024)} %param.7) | copy-start | bytes 49156
  2.7 0.7 %copy-start.3 = (s32[4096]{0:T(1024)S(1)}, s32[4096]{0:T(1024)}, u32[]{:S(2)}) copy-start(s32[4096]{0:T(1024)} %param.8) | copy-start | bytes 49156
  3.4 0.7 %copy-start.4 = (s32[4096]{0:T(1024)S(1)}, s32[4096]{0:T(1024)}, u32[]{:S(2)}) copy-start(s32[4096]{0:T(1024)} %param.9) | copy-start | bytes 49156

commit v2 on v1

--- a/solution.py
+++ b/solution.py
@@ -44,7 +44,7 @@
     frames, dead_hbm, band_hbm, label_hbm, valid_hbm,
     out,
     dead, band, label, valid, arrived, rate, smooth, outgoing,
-    lhs, gsend, grecv, gown, hsend, hrecv, hown, tsend, trecv,
+    gram, sums_ref, sums_t, gsend, grecv, gown, hsend, hrecv, hown, tsend, trecv,
     stat1, stat2, stat3, statg2, statg3, spread, spread_t,
     fsend, frecv,
     par_sem, own_sem, a2a_send, a2a_recv, sib_send, sib_recv,
@@ -72,6 +72,16 @@
 
     sibling = (x * CORES + (1 - c), p)
 
+    pending = []
+
+    def launch(copy):
+        copy.start()
+        pending.append(copy)
+
+    def finish():
+        for copy in pending:
+            copy.wait_send()
+
     barrier = pltpu.get_barrier_semaphore()
     for k in range(1, NDEV_FRAME):
         pl.semaphore_signal(barrier, inc=1, device_id=frame_peer((f + k) % NDEV_FRAME), device_id_type=MESH)
@@ -95,7 +105,7 @@
 
     for chunk in range(CHUNKS):
         for k in range(1, NDEV_FRAME):
-            a2a_copy(k, chunk).start()
+            launch(a2a_copy(k, chunk))
         own_copy(chunk).start()
     params = [
         pltpu.make_async_copy(src, dst, par_sem.at[n])
@@ -113,11 +123,34 @@
     def sib_copy(chunk):
         return remote(
             outgoing.at[chunk],
-            smooth.at[:, pl.ds(OWN_PIX + chunk * LANES, LANES)],
+            smooth.at[:, pl.ds((2 * chunk + 1) * LANES, LANES)],
             sib_send.at[chunk],
             sib_recv.at[chunk],
             sibling,
         )
+
+    contract_last = (((1,), (1,)), ((), ()))
+
+    def accumulate(chunk):
+        lanes = slice(2 * chunk * LANES, 2 * (chunk + 1) * LANES)
+        sib_copy(chunk).wait_recv()
+        part = lax.dot_general(
+            jnp.ones((8, 2 * LANES), jnp.bfloat16), smooth[:, lanes], contract_last, preferred_element_type=jnp.float32
+        )
+        sums_ref[...] = part if chunk == 0 else sums_ref[...] + part
+
+        def columns(n, _):
+            cols = pl.ds(pl.multiple_of(n * TILE, TILE), TILE)
+            product = lax.dot_general(
+                smooth[:, lanes], smooth[cols, lanes], contract_last, preferred_element_type=jnp.float32
+            )
+            if chunk == 0:
+                gram[:, cols] = product
+            else:
+                gram[:, cols] += product
+            return 0
+
+        lax.fori_loop(0, NFRAMES // TILE, columns, 0)
 
     for chunk in range(CHUNKS):
         own_copy(chunk).wait()
@@ -157,7 +190,7 @@
 
         def put(start, value):
             rows = pl.ds(start, GROUP)
-            smooth[rows, chunk * LANES : (chunk + 1) * LANES] = (value * mine).astype(jnp.bfloat16)
+            smooth[rows, 2 * chunk * LANES : (2 * chunk + 1) * LANES] = (value * mine).astype(jnp.bfloat16)
             outgoing[chunk, rows, :] = (value * other).astype(jnp.bfloat16)
 
         def inside(block, _):
@@ -170,19 +203,17 @@
             span = jnp.minimum(frame + width, NFRAMES - 1) - jnp.maximum(frame - width, 0) + 1
             put(start, window(start) / span.astype(jnp.float32))
         lax.fori_loop(1, NFRAMES // GROUP - 1, inside, 0)
-        sib_copy(chunk).start()
+        launch(sib_copy(chunk))
+        if chunk:
+            accumulate(chunk - 1)
 
     chip_label = label[pl.ds(pl.multiple_of(x * (CHIP_PIX // LANES), 8), CHIP_PIX // LANES), :]
     chip_valid = valid[pl.ds(pl.multiple_of(x * (CHIP_PIX // LANES), 8), CHIP_PIX // LANES), :]
     held = jnp.sum(jnp.where((chip_label == c) & (chip_valid == 1), 1.0, 0.0), axis=(0, 1), keepdims=True)
 
-    for chunk in range(CHUNKS):
-        sib_copy(chunk).wait_recv()
-
-    contract_last = (((1,), (1,)), ((), ()))
-    sums = lax.dot_general(
-        jnp.ones((8, CHIP_PIX), jnp.bfloat16), smooth[...], contract_last, preferred_element_type=jnp.float32
-    )[0:1, :]
+    accumulate(CHUNKS - 1)
+    sums = sums_ref[0:1, :]
+    sums_t[...] = jnp.transpose(sums_ref[...] / jnp.maximum(held, 1.0))
     stat1[a1, 0:1, :] = sums
     stat1[a1, 1:2, :] = jnp.broadcast_to(held, (1, NFRAMES))
 
@@ -191,7 +222,7 @@
         return remote(stat1.at[a1], stat1.at[a1], s1_send.at[k], s1_recv.at[a1], first_peer(to))
 
     for k in range(1, 4):
-        stat1_copy(k).start()
+        launch(stat1_copy(k))
 
     def group_start(a, g):
         second, core = g // CORES, g % CORES
@@ -206,74 +237,56 @@
             gsend.at[to, rows, :], grecv.at[a1, rows, :], g_send.at[k, sub], g_recv.at[a1, sub], first_peer(to)
         )
 
-    ones = jnp.ones((CHIP_PIX, LANES), jnp.bfloat16)
     for k in (1, 2, 3, 0):
         to = (a1 + k) % 4
         for g in range(8):
-            lhs[g * GROUP : (g + 1) * GROUP, :] = smooth[pl.ds(group_start(to, g), GROUP), :]
-        column = jnp.dot(lhs[...], ones, preferred_element_type=jnp.float32) / jnp.maximum(held, 1.0)
-
-        def tile(n, _):
-            cols = pl.ds(pl.multiple_of(n * TILE, TILE), TILE)
-            product = lax.dot_general(
-                lhs[...], smooth[cols, :], contract_last, preferred_element_type=jnp.float32
-            )
-            gown[:, cols] = product
-            return 0
-
-        lax.fori_loop(0, NFRAMES // TILE, tile, 0)
-        for n in range(NFRAMES // LANES):
-            cols = slice(n * LANES, (n + 1) * LANES)
-            centred = gown[:, cols] - column * sums[:, cols]
-            if k:
-                gsend[to, :, cols] = centred.astype(jnp.bfloat16)
-            else:
-                gown[:, cols] = centred
+            start = group_start(to, g)
+            column = jnp.broadcast_to(sums_t[pl.ds(start, GROUP), 0:1], (GROUP, LANES))
+            rows = pl.ds(g * GROUP, GROUP)
+            for n in range(NFRAMES // LANES):
+                cols = slice(n * LANES, (n + 1) * LANES)
+                centred = gram[pl.ds(start, GROUP), cols] - column * sums[:, cols]
+                if k:
+                    gsend[to, rows, cols] = centred.astype(jnp.bfloat16)
+                else:
+                    gown[rows, cols] = centred
         if k:
             for j in (1, 2, 3, 0):
-                g_copy(k, (a2 + j) % 4).start()
+                launch(g_copy(k, (a2 + j) % 4))
 
     for k in range(1, 4):
         source = (a1 + k) % 4
         remote(stat1.at[source], stat1.at[source], s1_send.at[k], s1_recv.at[source], first_peer(source)).wait_recv()
     statg2[...] = stat1[0] + stat1[1] + stat1[2] + stat1[3]
+    stat2[a2] = statg2[...]
 
     def stat2_copy(k):
         return remote(statg2, stat2.at[a2], s2_send.at[k], s2_recv.at[a2], second_peer((a2 + k) % 4))
 
     for k in range(1, 4):
-        stat2_copy(k).start()
-    total = statg2[...]
-    for k in range(1, 4):
-        source = (a2 + k) % 4
-        remote(statg2, stat2.at[source], s2_send.at[k], s2_recv.at[source], second_peer(source)).wait_recv()
-        total = total + stat2[source]
-    statg3[...] = total
-
+        launch(stat2_copy(k))
     def stat3_copy(k):
         return remote(statg3, stat3.at[z], s3_send.at[k], s3_recv.at[z], z_peer((z + k) % NZ))
 
-    for k in range(1, NZ):
-        stat3_copy(k).start()
-    for k in range(1, NZ):
-        source = (z + k) % NZ
-        remote(statg3, stat3.at[source], s3_send.at[k], s3_recv.at[source], z_peer(source)).wait_recv()
-        total = total + stat3[source]
-    counts = total[1:2, :]
-    mean = total[0:1, :] / counts
+    def between(stat, members):
+        group = stat[0]
+        for k in range(1, members):
+            group = group + stat[k]
+        mean = group[0:1, :] / jnp.maximum(group[1:2, :], 1.0)
+        for k in range(members):
+            spread[k : k + 1, :] = stat[k, 0:1, :] / jnp.maximum(stat[k, 1:2, :], 1.0) - mean
+        spread_t[...] = jnp.transpose(spread[...])
+        for k in range(members):
+            spread[k : k + 1, :] = spread[k : k + 1, :] * stat[k, 1:2, :]
+        return group
+
+    def outer(rows):
+        return jnp.dot(rows, spread[...], preferred_element_type=jnp.float32, precision=lax.Precision.HIGHEST)
 
     spread[...] = jnp.zeros_like(spread)
-    for k in range(4):
-        spread[k : k + 1, :] = stat1[k, 0:1, :] / jnp.maximum(stat1[k, 1:2, :], 1.0) - mean
-    spread_t[...] = jnp.transpose(spread[...])
-    for k in range(4):
-        spread[k : k + 1, :] = spread[k : k + 1, :] * stat1[k, 1:2, :]
+    between(stat1, 4)
     for g in range(8):
-        rows = pl.ds(g * GROUP, GROUP)
-        gown[rows, :] += jnp.dot(
-            spread_t[pl.ds(group_start(a1, g), GROUP), :], spread[...],
-            preferred_element_type=jnp.float32, precision=lax.Precision.HIGHEST,
-        )
+        gown[g * GROUP : (g + 1) * GROUP, :] += outer(spread_t[pl.ds(group_start(a1, g), GROUP), :])
 
     def h_copy(k):
         to = (a2 + k) % 4
@@ -293,10 +306,22 @@
             value = value + grecv[(a1 + k) % 4, rows, :].astype(jnp.float32)
         if j:
             hsend[sub] = value.astype(jnp.bfloat16)
-            h_copy(j).start()
+            launch(h_copy(j))
         else:
             hown[...] = value
 
+    for k in range(1, 4):
+        source = (a2 + k) % 4
+        remote(statg2, stat2.at[source], s2_send.at[k], s2_recv.at[source], second_peer(source)).wait_recv()
+    statg3[...] = stat2[0] + stat2[1] + stat2[2] + stat2[3]
+    stat3[z] = statg3[...]
+    for k in range(1, NZ):
+        launch(stat3_copy(k))
+    between(stat2, 4)
+    for core in range(CORES):
+        hown[core * GROUP : (core + 1) * GROUP, :] += outer(
+            spread_t[pl.ds(group_start(a1, a2 * CORES + core), GROUP), :]
+        )
     for k in range(1, 4):
         source = (a2 + k) % 4
         remote(hsend.at[source], hrecv.at[source], h_send.at[k], h_recv.at[source], second_peer(source)).wait_recv()
@@ -318,8 +343,18 @@
         return remote(tsend.at[to], trecv.at[z], t_send.at[k], t_recv.at[z], z_peer(to))
 
     for k in range(1, NZ):
-        t_copy(k).start()
-    value = tsend[z].astype(jnp.float32)
+        launch(t_copy(k))
+    for k in range(1, NZ):
+        source = (z + k) % NZ
+        remote(statg3, stat3.at[source], s3_send.at[k], s3_recv.at[source], z_peer(source)).wait_recv()
+    counts = between(stat3, NZ)[1:2, :]
+    halves = [
+        spread_t[pl.ds(pl.multiple_of(group_start(a1, a2 * CORES + core) + z // 2 * 8, 8), 8), :] for core in range(CORES)
+    ]
+    even = z % 2 == 0
+    value = tsend[z].astype(jnp.float32) + outer(
+        jnp.concatenate([jnp.where(even, half[0:own_rows], half[own_rows : 2 * own_rows]) for half in halves], axis=0)
+    )
     for k in range(1, NZ):
         source = (z + k) % NZ
         remote(tsend.at[source], trecv.at[source], t_send.at[k], t_recv.at[source], z_peer(source)).wait_recv()
@@ -329,25 +364,12 @@
     low, high = value[0:own_rows, :], value[own_rows : 2 * own_rows, :]
     fsend[...] = jnp.where(c == 0, high, low)
     last = remote(fsend, frecv, f_send, f_recv, sibling)
-    last.start()
+    launch(last)
     out[c] = jnp.where(c == 0, low, high)
     last.wait_recv()
     out[1 - c] = frecv[...]
 
-    for chunk in range(CHUNKS):
-        for k in range(1, NDEV_FRAME):
-            a2a_copy(k, chunk).wait_send()
-        sib_copy(chunk).wait_send()
-    for k in range(1, 4):
-        stat1_copy(k).wait_send()
-        stat2_copy(k).wait_send()
-        h_copy(k).wait_send()
-        for sub in range(4):
-            g_copy(k, sub).wait_send()
-    for k in range(1, NZ):
-        stat3_copy(k).wait_send()
-        t_copy(k).wait_send()
-    last.wait_send()
+    finish()
 
 
 def shards(frames, dead_time, band_width, cycle_label, valid):
@@ -356,7 +378,7 @@
     own_rows = GROUP // NZ
     dma = pltpu.SemaphoreType.DMA
     f32, bf16 = jnp.float32, jnp.bfloat16
-    any_space = pl.BlockSpec(memory_space=pl.ANY)
+    any_space = pl.BlockSpec(memory_space=pltpu.HBM)
     vmem = pltpu.VMEM
     out = pl.pallas_call(
         kernel,
@@ -372,7 +394,9 @@
             vmem((PAD + NFRAMES + PAD, LANES), f32),
             vmem((NFRAMES, CHIP_PIX), bf16),
             vmem((CHUNKS, NFRAMES, LANES), bf16),
-            vmem((CLASS_ROWS, CHIP_PIX), bf16),
+            vmem((NFRAMES, NFRAMES), f32),
+            vmem((8, NFRAMES), f32),
+            vmem((NFRAMES, 8), f32),
             vmem((4, CLASS_ROWS, NFRAMES), bf16),
             vmem((4, CLASS_ROWS, NFRAMES), bf16),
             vmem((CLASS_ROWS, NFRAMES), f32),
@@ -403,7 +427,7 @@
             dma, dma,
         ],
         compiler_params=pltpu.CompilerParams(
-            collective_id=0, has_side_effects=True, vmem_limit_bytes=48 * 2**20
+            collective_id=0, has_side_effects=True, vmem_limit_bytes=60 * 2**20
         ),
     )(frames, *flat)
     return jnp.transpose(out, (1, 0, 2))

time: 64.1 us -> 57.9 us (0.903)
  local copies, waits for them, and re-layouts: 4.73 us -> 1.4 us
  Pallas kernels: 58.9 us -> 56.3 us
    unnamed x10 -> x0, local copies, waits for them, and re-layouts: 4.09 us -> none
    pallas_call x1, Pallas kernels: 58.9 us -> 56.3 us  [shards(): pl.pallas_call(kernel, out_shape=jax.ShapeDtypeStruct((CYCLES, own_rows,...]
    transpose x1, local copies, waits for them, and re-layouts: 0.64 us -> 1.4 us  [shards(): return jnp.transpose(out, (1, 0, 2))]
where the time goes in v2:
time: 57.9 us; the launch traced here: 57.7 us
  Pallas kernels  56.3 us (97%)
  local copies, waits for them, and re-layouts  1.4 us (2%)
    pallas_call x1, Pallas kernels, shards(): pl.pallas_call(kernel, out_shape=jax.ShapeDtypeStruct((CYCLES, own_rows,...  56.3 us
    transpose x1, local copies, waits for them, and re-layouts, shards(): return jnp.transpose(out, (1, 0, 2))  1.4 us

profile of v2, /device:TPU:1, one launch (start us, length us, event | category | flops | bytes accessed | tf_op | source)
XLA Modules:
  0.0 57.7 jit_solution(9304645767278367504)
XLA Ops:
  0.0 56.3 %shard_map.55 = f32[2,4,1024]{2,1,0:T(4,128)} custom-call(bf16[128,4096]{1,0:T(8,128)(2,1)} %frames.1, f32[32,128]{1,0:T(8,128)} %bitcast.6, s32[32,128]{1,0:T(8,128)} %bitcast.7, s32[32,128]{1,0:T(8,128)} %bitcast.8, s32[32,128]{1,0:T(8,128)} %bitcast.9), custom_call_target="tpu_custom_call" | custom-call | tf_op jit(solution)/shard_map/pallas_call | solution.py:383
  56.3 1.4 %copy.6 = f32[4,2,1024]{2,1,0:T(2,128)} copy(f32[4,2,1024]{2,0,1:T(4,128)} %bitcast.5) | data formatting | bytes 65536 | tf_op jit(solution)/shard_map/transpose | solution.py:433

commit v3 on v2

--- a/solution.py
+++ b/solution.py
@@ -26,7 +26,7 @@
 CLASS_ROWS = NFRAMES // 4
 SUB_ROWS = CLASS_ROWS // 4
 PAD = BAND
-TILE = 256
+TILE = 512
 
 
 def remote(src, dst, send_sem, recv_sem, device):
@@ -46,10 +46,9 @@
     dead, band, label, valid, arrived, rate, smooth, outgoing,
     gram, sums_ref, sums_t, gsend, grecv, gown, hsend, hrecv, hown, tsend, trecv,
     stat1, stat2, stat3, statg2, statg3, spread, spread_t,
-    fsend, frecv,
     par_sem, own_sem, a2a_send, a2a_recv, sib_send, sib_recv,
     s1_send, s1_recv, s2_send, s2_recv, s3_send, s3_recv,
-    g_send, g_recv, h_send, h_recv, t_send, t_recv, f_send, f_recv,
+    g_send, g_recv, h_send, h_recv, t_send, t_recv,
 ):
     f = lax.axis_index("frame")
     p = lax.axis_index("pixel")
@@ -88,8 +87,11 @@
     for k in range(1, NY):
         pl.semaphore_signal(barrier, inc=1, device_id=(f, ((y + k) % NY) * NZ + z), device_id_type=MESH)
     for k in range(1, NZ):
-        pl.semaphore_signal(barrier, inc=1, device_id=z_peer((z + k) % NZ), device_id_type=MESH)
-    pl.semaphore_wait(barrier, NDEV_FRAME - 1 + NY - 1 + NZ - 1)
+        for core in range(CORES):
+            pl.semaphore_signal(
+                barrier, inc=1, device_id=(x * CORES + core, y * NZ + (z + k) % NZ), device_id_type=MESH
+            )
+    pl.semaphore_wait(barrier, NDEV_FRAME - 1 + NY - 1 + CORES * (NZ - 1))
 
     def piece(owner, chunk):
         return frames.at[:, pl.ds(pl.multiple_of(owner * OWN_PIX + chunk * LANES, LANES), LANES)]
@@ -139,18 +141,12 @@
         )
         sums_ref[...] = part if chunk == 0 else sums_ref[...] + part
 
-        def columns(n, _):
-            cols = pl.ds(pl.multiple_of(n * TILE, TILE), TILE)
+        for n in range(NFRAMES // TILE):
+            cols = slice(n * TILE, (n + 1) * TILE)
             product = lax.dot_general(
                 smooth[:, lanes], smooth[cols, lanes], contract_last, preferred_element_type=jnp.float32
             )
-            if chunk == 0:
-                gram[:, cols] = product
-            else:
-                gram[:, cols] += product
-            return 0
-
-        lax.fori_loop(0, NFRAMES // TILE, columns, 0)
+            gram[:, cols] = product if chunk == 0 else gram[:, cols] + product
 
     for chunk in range(CHUNKS):
         own_copy(chunk).wait()
@@ -250,10 +246,10 @@
                     gsend[to, rows, cols] = centred.astype(jnp.bfloat16)
                 else:
                     gown[rows, cols] = centred
-        if k:
-            for j in (1, 2, 3, 0):
-                launch(g_copy(k, (a2 + j) % 4))
-
+
+    for j in (1, 2, 3, 0):
+        for k in (2, 1, 3):
+            launch(g_copy(k, (a2 + j) % 4))
     for k in range(1, 4):
         source = (a1 + k) % 4
         remote(stat1.at[source], stat1.at[source], s1_send.at[k], s1_recv.at[source], first_peer(source)).wait_recv()
@@ -268,23 +264,19 @@
     def stat3_copy(k):
         return remote(statg3, stat3.at[z], s3_send.at[k], s3_recv.at[z], z_peer((z + k) % NZ))
 
-    def between(stat, members):
-        group = stat[0]
-        for k in range(1, members):
-            group = group + stat[k]
+    def between(stat, group):
         mean = group[0:1, :] / jnp.maximum(group[1:2, :], 1.0)
-        for k in range(members):
+        for k in range(4):
             spread[k : k + 1, :] = stat[k, 0:1, :] / jnp.maximum(stat[k, 1:2, :], 1.0) - mean
         spread_t[...] = jnp.transpose(spread[...])
-        for k in range(members):
+        for k in range(4):
             spread[k : k + 1, :] = spread[k : k + 1, :] * stat[k, 1:2, :]
-        return group
 
     def outer(rows):
         return jnp.dot(rows, spread[...], preferred_element_type=jnp.float32, precision=lax.Precision.HIGHEST)
 
     spread[...] = jnp.zeros_like(spread)
-    between(stat1, 4)
+    between(stat1, statg2[...])
     for g in range(8):
         gown[g * GROUP : (g + 1) * GROUP, :] += outer(spread_t[pl.ds(group_start(a1, g), GROUP), :])
 
@@ -301,6 +293,15 @@
                 gsend.at[source, rows, :], grecv.at[source, rows, :], g_send.at[k, sub], g_recv.at[source, sub],
                 first_peer(source),
             ).wait_recv()
+        if j == 3:
+            for k in range(1, 4):
+                source = (a2 + k) % 4
+                remote(
+                    statg2, stat2.at[source], s2_send.at[k], s2_recv.at[source], second_peer(source)
+                ).wait_recv()
+            statg3[...] = stat2[0] + stat2[1] + stat2[2] + stat2[3]
+            for k in range(1, NZ):
+                launch(stat3_copy(k))
         value = gown[rows, :]
         for k in range(1, 4):
             value = value + grecv[(a1 + k) % 4, rows, :].astype(jnp.float32)
@@ -310,64 +311,56 @@
         else:
             hown[...] = value
 
-    for k in range(1, 4):
-        source = (a2 + k) % 4
-        remote(statg2, stat2.at[source], s2_send.at[k], s2_recv.at[source], second_peer(source)).wait_recv()
-    statg3[...] = stat2[0] + stat2[1] + stat2[2] + stat2[3]
-    stat3[z] = statg3[...]
+    everything = statg3[...]
     for k in range(1, NZ):
-        launch(stat3_copy(k))
-    between(stat2, 4)
+        source = (z + k) % NZ
+        remote(statg3, stat3.at[source], s3_send.at[k], s3_recv.at[source], z_peer(source)).wait_recv()
+        everything = everything + stat3[source]
+    between(stat2, everything)
     for core in range(CORES):
         hown[core * GROUP : (core + 1) * GROUP, :] += outer(
             spread_t[pl.ds(group_start(a1, a2 * CORES + core), GROUP), :]
         )
+
     for k in range(1, 4):
         source = (a2 + k) % 4
         remote(hsend.at[source], hrecv.at[source], h_send.at[k], h_recv.at[source], second_peer(source)).wait_recv()
     value = hown[...]
     for k in range(1, 4):
         value = value + hrecv[(a2 + k) % 4].astype(jnp.float32)
-    hown[...] = value
+    hown[...] = value / everything[1:2, :]
     own_rows = GROUP // NZ
 
     for other_z in range(NZ):
-        rows = jnp.concatenate(
-            [hown[core * GROUP + other_z * own_rows : core * GROUP + (other_z + 1) * own_rows, :] for core in range(CORES)],
-            axis=0,
-        )
-        tsend[other_z] = rows.astype(jnp.bfloat16)
-
-    def t_copy(k):
-        to = (z + k) % NZ
-        return remote(tsend.at[to], trecv.at[z], t_send.at[k], t_recv.at[z], z_peer(to))
-
-    for k in range(1, NZ):
-        launch(t_copy(k))
-    for k in range(1, NZ):
-        source = (z + k) % NZ
-        remote(statg3, stat3.at[source], s3_send.at[k], s3_recv.at[source], z_peer(source)).wait_recv()
-    counts = between(stat3, NZ)[1:2, :]
-    halves = [
-        spread_t[pl.ds(pl.multiple_of(group_start(a1, a2 * CORES + core) + z // 2 * 8, 8), 8), :] for core in range(CORES)
-    ]
-    even = z % 2 == 0
-    value = tsend[z].astype(jnp.float32) + outer(
-        jnp.concatenate([jnp.where(even, half[0:own_rows], half[own_rows : 2 * own_rows]) for half in halves], axis=0)
-    )
-    for k in range(1, NZ):
-        source = (z + k) % NZ
-        remote(tsend.at[source], trecv.at[source], t_send.at[k], t_recv.at[source], z_peer(source)).wait_recv()
-        value = value + trecv[source].astype(jnp.float32)
-    value = value / counts
-
-    low, high = value[0:own_rows, :], value[own_rows : 2 * own_rows, :]
-    fsend[...] = jnp.where(c == 0, high, low)
-    last = remote(fsend, frecv, f_send, f_recv, sibling)
-    launch(last)
-    out[c] = jnp.where(c == 0, low, high)
-    last.wait_recv()
-    out[1 - c] = frecv[...]
+        for core in range(CORES):
+            start = core * GROUP + other_z * own_rows
+            tsend[other_z, core] = hown[start : start + own_rows, :].astype(jnp.bfloat16)
+
+    def t_copy(k, flip):
+        to, core = (z + k) % NZ, (c + flip) % CORES
+        return remote(
+            tsend.at[to, core], trecv.at[c, z], t_send.at[k, flip], t_recv.at[c, z],
+            (x * CORES + core, y * NZ + to),
+        )
+
+    for k in range(NZ):
+        for flip in range(CORES):
+            if k or flip:
+                launch(t_copy(k, flip))
+    trecv[c, z] = tsend[z, c]
+    for k in range(NZ):
+        for flip in range(CORES):
+            if k or flip:
+                source, core = (z + k) % NZ, (c + flip) % CORES
+                remote(
+                    tsend.at[source, core], trecv.at[core, source], t_send.at[k, flip], t_recv.at[core, source],
+                    (x * CORES + core, y * NZ + source),
+                ).wait_recv()
+    for core in range(CORES):
+        value = trecv[core, 0].astype(jnp.float32)
+        for k in range(1, NZ):
+            value = value + trecv[core, k].astype(jnp.float32)
+        out[core] = value
 
     finish()
 
@@ -403,8 +396,8 @@
             vmem((4, SUB_ROWS, NFRAMES), bf16),
             vmem((4, SUB_ROWS, NFRAMES), bf16),
             vmem((SUB_ROWS, NFRAMES), f32),
-            vmem((NZ, CORES * own_rows, NFRAMES), bf16),
-            vmem((NZ, CORES * own_rows, NFRAMES), bf16),
+            vmem((NZ, CORES, own_rows, NFRAMES), bf16),
+            vmem((CORES, NZ, own_rows, NFRAMES), bf16),
             vmem((4, 2, NFRAMES), f32),
             vmem((4, 2, NFRAMES), f32),
             vmem((NZ, 2, NFRAMES), f32),
@@ -412,8 +405,6 @@
             vmem((2, NFRAMES), f32),
             vmem((8, NFRAMES), f32),
             vmem((NFRAMES, 8), f32),
-            vmem((own_rows, NFRAMES), f32),
-            vmem((own_rows, NFRAMES), f32),
             dma((4,)),
             dma((CHUNKS,)),
             dma((CHUNKS, NDEV_FRAME)), dma((CHUNKS, NDEV_FRAME)),
@@ -423,8 +414,7 @@
             dma((NZ,)), dma((NZ,)),
             dma((4, 4)), dma((4, 4)),
             dma((4,)), dma((4,)),
-            dma((NZ,)), dma((NZ,)),
-            dma, dma,
+            dma((NZ, CORES)), dma((CORES, NZ)),
         ],
         compiler_params=pltpu.CompilerParams(
             collective_id=0, has_side_effects=True, vmem_limit_bytes=60 * 2**20

time: 57.9 us -> 58.8 us (1.016)
  Pallas kernels: 56.3 us -> 57.2 us
    pallas_call x1, Pallas kernels: 56.3 us -> 57.2 us  [shards(): pl.pallas_call(kernel, out_shape=jax.ShapeDtypeStruct((CYCLES, own_rows,...]
where the time goes in v3:
time: 58.8 us; the launch traced here: 58.6 us
  Pallas kernels  57.2 us (97%)
  local copies, waits for them, and re-layouts  1.4 us (2%)
    pallas_call x1, Pallas kernels, shards(): pl.pallas_call(kernel, out_shape=jax.ShapeDtypeStruct((CYCLES, own_rows,...  57.2 us
    transpose x1, local copies, waits for them, and re-layouts, shards(): return jnp.transpose(out, (1, 0, 2))  1.4 us

profile of v3, /device:TPU:1, one launch (start us, length us, event | category | flops | bytes accessed | tf_op | source)
XLA Modules:
  0.0 58.6 jit_solution(15853588205887739419)
XLA Ops:
  0.0 57.2 %shard_map.55 = f32[2,4,1024]{2,1,0:T(4,128)} custom-call(bf16[128,4096]{1,0:T(8,128)(2,1)} %frames.1, f32[32,128]{1,0:T(8,128)} %bitcast.6, s32[32,128]{1,0:T(8,128)} %bitcast.7, s32[32,128]{1,0:T(8,128)} %bitcast.8, s32[32,128]{1,0:T(8,128)} %bitcast.9), custom_call_target="tpu_custom_call" | custom-call | tf_op jit(solution)/shard_map/pallas_call | solution.py:376
  57.2 1.4 %copy.6 = f32[4,2,1024]{2,1,0:T(2,128)} copy(f32[4,2,1024]{2,0,1:T(4,128)} %bitcast.5) | data formatting | bytes 65536 | tf_op jit(solution)/shard_map/transpose | solution.py:423

commit v4 on v2

--- a/solution.py
+++ b/solution.py
@@ -26,7 +26,7 @@
 CLASS_ROWS = NFRAMES // 4
 SUB_ROWS = CLASS_ROWS // 4
 PAD = BAND
-TILE = 256
+TILE = 512
 
 
 def remote(src, dst, send_sem, recv_sem, device):
@@ -139,18 +139,12 @@
         )
         sums_ref[...] = part if chunk == 0 else sums_ref[...] + part
 
-        def columns(n, _):
-            cols = pl.ds(pl.multiple_of(n * TILE, TILE), TILE)
+        for n in range(NFRAMES // TILE):
+            cols = slice(n * TILE, (n + 1) * TILE)
             product = lax.dot_general(
                 smooth[:, lanes], smooth[cols, lanes], contract_last, preferred_element_type=jnp.float32
             )
-            if chunk == 0:
-                gram[:, cols] = product
-            else:
-                gram[:, cols] += product
-            return 0
-
-        lax.fori_loop(0, NFRAMES // TILE, columns, 0)
+            gram[:, cols] = product if chunk == 0 else gram[:, cols] + product
 
     for chunk in range(CHUNKS):
         own_copy(chunk).wait()
@@ -250,10 +244,10 @@
                     gsend[to, rows, cols] = centred.astype(jnp.bfloat16)
                 else:
                     gown[rows, cols] = centred
-        if k:
-            for j in (1, 2, 3, 0):
-                launch(g_copy(k, (a2 + j) % 4))
-
+
+    for j in (1, 2, 3, 0):
+        for k in (2, 1, 3):
+            launch(g_copy(k, (a2 + j) % 4))
     for k in range(1, 4):
         source = (a1 + k) % 4
         remote(stat1.at[source], stat1.at[source], s1_send.at[k], s1_recv.at[source], first_peer(source)).wait_recv()

time: 57.9 us -> 55.8 us (0.964)
  Pallas kernels: 56.3 us -> 54.2 us
    pallas_call x1, Pallas kernels: 56.3 us -> 54.2 us  [shards(): pl.pallas_call(kernel, out_shape=jax.ShapeDtypeStruct((CYCLES, own_rows,...]
where the time goes in v4:
time: 55.8 us; the launch traced here: 55.6 us
  Pallas kernels  54.2 us (97%)
  local copies, waits for them, and re-layouts  1.4 us (3%)
    pallas_call x1, Pallas kernels, shards(): pl.pallas_call(kernel, out_shape=jax.ShapeDtypeStruct((CYCLES, own_rows,...  54.2 us
    transpose x1, local copies, waits for them, and re-layouts, shards(): return jnp.transpose(out, (1, 0, 2))  1.4 us

profile of v4, /device:TPU:1, one launch (start us, length us, event | category | flops | bytes accessed | tf_op | source)
XLA Modules:
  0.0 55.6 jit_solution(6444528053453095288)
XLA Ops:
  0.0 54.2 %shard_map.55 = f32[2,4,1024]{2,1,0:T(4,128)} custom-call(bf16[128,4096]{1,0:T(8,128)(2,1)} %frames.1, f32[32,128]{1,0:T(8,128)} %bitcast.6, s32[32,128]{1,0:T(8,128)} %bitcast.7, s32[32,128]{1,0:T(8,128)} %bitcast.8, s32[32,128]{1,0:T(8,128)} %bitcast.9), custom_call_target="tpu_custom_call" | custom-call | tf_op jit(solution)/shard_map/pallas_call | solution.py:377
  54.2 1.4 %copy.6 = f32[4,2,1024]{2,1,0:T(2,128)} copy(f32[4,2,1024]{2,0,1:T(4,128)} %bitcast.5) | data formatting | bytes 65536 | tf_op jit(solution)/shard_map/transpose | solution.py:427

commit v5 on v4

--- a/solution.py
+++ b/solution.py
@@ -26,7 +26,8 @@
 CLASS_ROWS = NFRAMES // 4
 SUB_ROWS = CLASS_ROWS // 4
 PAD = BAND
-TILE = 512
+TILE = 256
+HELD = 640
 
 
 def remote(src, dst, send_sem, recv_sem, device):
@@ -46,10 +47,11 @@
     dead, band, label, valid, arrived, rate, smooth, outgoing,
     gram, sums_ref, sums_t, gsend, grecv, gown, hsend, hrecv, hown, tsend, trecv,
     stat1, stat2, stat3, statg2, statg3, spread, spread_t,
-    fsend, frecv,
+    fsend, frecv, m1_out, m1_in, m2_out, m2_in, permuted, ordered,
     par_sem, own_sem, a2a_send, a2a_recv, sib_send, sib_recv,
     s1_send, s1_recv, s2_send, s2_recv, s3_send, s3_recv,
     g_send, g_recv, h_send, h_recv, t_send, t_recv, f_send, f_recv,
+    m1_send, m1_recv, m2_send, m2_recv,
 ):
     f = lax.axis_index("frame")
     p = lax.axis_index("pixel")
@@ -58,11 +60,14 @@
     a1 = c * x + (1 - c) * y
     a2 = c * y + (1 - c) * x
 
+    def peer(a, b):
+        return ((c * a + (1 - c) * b) * CORES + c, (c * b + (1 - c) * a) * NZ + z)
+
     def first_peer(a):
-        return ((c * a + (1 - c) * x) * CORES + c, (c * y + (1 - c) * a) * NZ + z)
-
-    def second_peer(a):
-        return ((c * x + (1 - c) * a) * CORES + c, (c * a + (1 - c) * y) * NZ + z)
+        return peer(a, a2)
+
+    def second_peer(b):
+        return peer(a1, b)
 
     def z_peer(other):
         return (f, y * NZ + other)
@@ -89,7 +94,10 @@
         pl.semaphore_signal(barrier, inc=1, device_id=(f, ((y + k) % NY) * NZ + z), device_id_type=MESH)
     for k in range(1, NZ):
         pl.semaphore_signal(barrier, inc=1, device_id=z_peer((z + k) % NZ), device_id_type=MESH)
-    pl.semaphore_wait(barrier, NDEV_FRAME - 1 + NY - 1 + NZ - 1)
+    for k in range(1, 4):
+        for n in range(1, 4):
+            pl.semaphore_signal(barrier, inc=1, device_id=peer((a1 + k) % 4, (a2 + n) % 4), device_id_type=MESH)
+    pl.semaphore_wait(barrier, NDEV_FRAME - 1 + NY - 1 + NZ - 1 + 9)
 
     def piece(owner, chunk):
         return frames.at[:, pl.ds(pl.multiple_of(owner * OWN_PIX + chunk * LANES, LANES), LANES)]
@@ -139,12 +147,13 @@
         )
         sums_ref[...] = part if chunk == 0 else sums_ref[...] + part
 
-        for n in range(NFRAMES // TILE):
-            cols = slice(n * TILE, (n + 1) * TILE)
-            product = lax.dot_general(
-                smooth[:, lanes], smooth[cols, lanes], contract_last, preferred_element_type=jnp.float32
-            )
-            gram[:, cols] = product if chunk == 0 else gram[:, cols] + product
+        for m in range(4):
+            for n in (m, (m + 1) % 4, (m + 2) % 4):
+                rows, cols = slice(m * TILE, (m + 1) * TILE), slice(n * TILE, (n + 1) * TILE)
+                product = lax.dot_general(
+                    smooth[rows, lanes], smooth[cols, lanes], contract_last, preferred_element_type=jnp.float32
+                )
+                gram[rows, cols] = product if chunk == 0 else gram[rows, cols] + product
 
     for chunk in range(CHUNKS):
         own_copy(chunk).wait()
@@ -182,20 +191,22 @@
                 )
             return total
 
-        def put(start, value):
-            rows = pl.ds(start, GROUP)
-            smooth[rows, 2 * chunk * LANES : (2 * chunk + 1) * LANES] = (value * mine).astype(jnp.bfloat16)
-            outgoing[chunk, rows, :] = (value * other).astype(jnp.bfloat16)
+        def put(block, value):
+            row_x, core, row_y = block // 8, block // 4 % 2, block % 4
+            along_x, along_y = row_x * 8 + row_y * 2 + core, row_y * 8 + row_x * 2 + core
+            own_rows = pl.ds(pl.multiple_of((c * along_x + (1 - c) * along_y) * GROUP, GROUP), GROUP)
+            sib_rows = pl.ds(pl.multiple_of((c * along_y + (1 - c) * along_x) * GROUP, GROUP), GROUP)
+            smooth[own_rows, 2 * chunk * LANES : (2 * chunk + 1) * LANES] = (value * mine).astype(jnp.bfloat16)
+            outgoing[chunk, sib_rows, :] = (value * other).astype(jnp.bfloat16)
 
         def inside(block, _):
-            start = pl.multiple_of(block * GROUP, GROUP)
-            put(start, window(start) * full)
+            put(block, window(pl.multiple_of(block * GROUP, GROUP)) * full)
             return 0
 
         for start in (0, NFRAMES - GROUP):
             frame = start + lax.broadcasted_iota(jnp.int32, (GROUP, LANES), 0)
             span = jnp.minimum(frame + width, NFRAMES - 1) - jnp.maximum(frame - width, 0) + 1
-            put(start, window(start) / span.astype(jnp.float32))
+            put(start // GROUP, window(start) / span.astype(jnp.float32))
         lax.fori_loop(1, NFRAMES // GROUP - 1, inside, 0)
         launch(sib_copy(chunk))
         if chunk:
@@ -206,9 +217,8 @@
     held = jnp.sum(jnp.where((chip_label == c) & (chip_valid == 1), 1.0, 0.0), axis=(0, 1), keepdims=True)
 
     accumulate(CHUNKS - 1)
-    sums = sums_ref[0:1, :]
     sums_t[...] = jnp.transpose(sums_ref[...] / jnp.maximum(held, 1.0))
-    stat1[a1, 0:1, :] = sums
+    stat1[a1, 0:1, :] = sums_ref[0:1, :]
     stat1[a1, 1:2, :] = jnp.broadcast_to(held, (1, NFRAMES))
 
     def stat1_copy(k):
@@ -218,11 +228,12 @@
     for k in range(1, 4):
         launch(stat1_copy(k))
 
-    def group_start(a, g):
-        second, core = g // CORES, g % CORES
-        row_x = c * a + (1 - c) * second
-        row_y = c * second + (1 - c) * a
-        return pl.multiple_of((row_x * 8 + core * 4 + row_y) * GROUP, GROUP)
+    def lane(a, half):
+        return pl.ds(pl.multiple_of(((a1 + a) % 4 * 2 + half) * LANES, LANES), LANES)
+
+    def other_half(a, half):
+        high = a // 2
+        return (1 - half) * high + half * (1 - high)
 
     def g_copy(k, sub):
         to = (a1 + k) % 4
@@ -233,17 +244,17 @@
 
     for k in (1, 2, 3, 0):
         to = (a1 + k) % 4
-        for g in range(8):
-            start = group_start(to, g)
-            column = jnp.broadcast_to(sums_t[pl.ds(start, GROUP), 0:1], (GROUP, LANES))
-            rows = pl.ds(g * GROUP, GROUP)
-            for n in range(NFRAMES // LANES):
-                cols = slice(n * LANES, (n + 1) * LANES)
-                centred = gram[pl.ds(start, GROUP), cols] - column * sums[:, cols]
+        for half in range(2):
+            start = pl.multiple_of(to * CLASS_ROWS + half * LANES, LANES)
+            column = jnp.broadcast_to(sums_t[pl.ds(start, LANES), 0:1], (LANES, LANES))
+            rows = slice(half * LANES, (half + 1) * LANES)
+            held_lanes = [lane(k, 0), lane(k, 1), lane(k + 1, 0), lane(k + 1, 1), lane(k + 2, other_half(to, half))]
+            for n, cols in enumerate(held_lanes):
+                centred = gram[pl.ds(start, LANES), cols] - column * sums_ref[0:1, cols]
                 if k:
-                    gsend[to, rows, cols] = centred.astype(jnp.bfloat16)
+                    gsend[to, rows, n * LANES : (n + 1) * LANES] = centred.astype(jnp.bfloat16)
                 else:
-                    gown[rows, cols] = centred
+                    gown[rows, n * LANES : (n + 1) * LANES] = centred
 
     for j in (1, 2, 3, 0):
         for k in (2, 1, 3):
@@ -274,13 +285,18 @@
             spread[k : k + 1, :] = spread[k : k + 1, :] * stat[k, 1:2, :]
         return group
 
-    def outer(rows):
-        return jnp.dot(rows, spread[...], preferred_element_type=jnp.float32, precision=lax.Precision.HIGHEST)
+    def outer(rows, cols):
+        return jnp.dot(rows, spread[:, cols], preferred_element_type=jnp.float32, precision=lax.Precision.HIGHEST)
 
     spread[...] = jnp.zeros_like(spread)
     between(stat1, 4)
-    for g in range(8):
-        gown[g * GROUP : (g + 1) * GROUP, :] += outer(spread_t[pl.ds(group_start(a1, g), GROUP), :])
+    own_start = pl.multiple_of(a1 * CLASS_ROWS, CLASS_ROWS)
+    for n in range(4):
+        gown[:, n * LANES : (n + 1) * LANES] += outer(spread_t[pl.ds(own_start, CLASS_ROWS), :], lane(n // 2, n % 2))
+    for half in range(2):
+        gown[half * LANES : (half + 1) * LANES, 4 * LANES :] += outer(
+            spread_t[pl.ds(own_start + half * LANES, LANES), :], lane(2, other_half(a1, half))
+        )
 
     def h_copy(k):
         to = (a2 + k) % 4
@@ -298,11 +314,31 @@
         value = gown[rows, :]
         for k in range(1, 4):
             value = value + grecv[(a1 + k) % 4, rows, :].astype(jnp.float32)
+        gown[rows, :] = value
         if j:
             hsend[sub] = value.astype(jnp.bfloat16)
             launch(h_copy(j))
-        else:
-            hown[...] = value
+
+    def mirror_copy(n):
+        return remote(
+            m1_out.at[n], m1_in.at[a2], m1_send.at[n], m1_recv.at[a2], peer((a1 + 1) % 4, n)
+        )
+
+    def half_copy(n):
+        return remote(
+            m2_out.at[n], m2_in.at[a2], m2_send.at[n], m2_recv.at[a2], peer((a1 + 2) % 4, n)
+        )
+
+    mirror = jnp.transpose(gown[:, 2 * LANES : 4 * LANES]).astype(jnp.bfloat16)
+    for n in range(4):
+        m1_out[n] = mirror[n * SUB_ROWS : (n + 1) * SUB_ROWS, :]
+        launch(mirror_copy(n))
+    for half in range(2):
+        mirror = jnp.transpose(gown[half * LANES : (half + 1) * LANES, 4 * LANES :]).astype(jnp.bfloat16)
+        for n in range(2):
+            m2_out[other_half(a1, half) * 2 + n] = mirror[n * SUB_ROWS : (n + 1) * SUB_ROWS, :]
+    for n in range(4):
+        launch(half_copy(n))
 
     for k in range(1, 4):
         source = (a2 + k) % 4
@@ -312,17 +348,30 @@
     for k in range(1, NZ):
         launch(stat3_copy(k))
     between(stat2, 4)
-    for core in range(CORES):
-        hown[core * GROUP : (core + 1) * GROUP, :] += outer(
-            spread_t[pl.ds(group_start(a1, a2 * CORES + core), GROUP), :]
-        )
+    row_start = pl.multiple_of(a1 * CLASS_ROWS + a2 * SUB_ROWS, SUB_ROWS)
+    hown[...] = outer(spread_t[pl.ds(row_start, SUB_ROWS), :], slice(None))
     for k in range(1, 4):
         source = (a2 + k) % 4
         remote(hsend.at[source], hrecv.at[source], h_send.at[k], h_recv.at[source], second_peer(source)).wait_recv()
-    value = hown[...]
+    value = gown[pl.ds(pl.multiple_of(a2 * SUB_ROWS, SUB_ROWS), SUB_ROWS), :]
     for k in range(1, 4):
         value = value + hrecv[(a2 + k) % 4].astype(jnp.float32)
-    hown[...] = value
+    own_half = other_half(a1, a2 // 2)
+    for n, cols in enumerate((lane(0, 0), lane(0, 1), lane(1, 0), lane(1, 1), lane(2, own_half))):
+        hown[:, cols] += value[:, n * LANES : (n + 1) * LANES]
+    for n in range(4):
+        remote(m1_out.at[n], m1_in.at[n], m1_send.at[n], m1_recv.at[n], peer((a1 + 3) % 4, n)).wait_recv()
+    value = m1_in[0].astype(jnp.float32)
+    for n in range(1, 4):
+        value = value + m1_in[n].astype(jnp.float32)
+    hown[:, lane(3, 0)] += value[:, 0:LANES]
+    hown[:, lane(3, 1)] += value[:, LANES:]
+    for n in range(4):
+        remote(m2_out.at[n], m2_in.at[n], m2_send.at[n], m2_recv.at[n], peer((a1 + 2) % 4, n)).wait_recv()
+    value = m2_in[0].astype(jnp.float32)
+    for n in range(1, 4):
+        value = value + m2_in[n].astype(jnp.float32)
+    hown[:, lane(2, 1 - own_half)] += value
     own_rows = GROUP // NZ
 
     for other_z in range(NZ):
@@ -343,17 +392,31 @@
         remote(statg3, stat3.at[source], s3_send.at[k], s3_recv.at[source], z_peer(source)).wait_recv()
     counts = between(stat3, NZ)[1:2, :]
     halves = [
-        spread_t[pl.ds(pl.multiple_of(group_start(a1, a2 * CORES + core) + z // 2 * 8, 8), 8), :] for core in range(CORES)
+        spread_t[pl.ds(pl.multiple_of(row_start + core * GROUP + z // 2 * 8, 8), 8), :] for core in range(CORES)
     ]
     even = z % 2 == 0
     value = tsend[z].astype(jnp.float32) + outer(
-        jnp.concatenate([jnp.where(even, half[0:own_rows], half[own_rows : 2 * own_rows]) for half in halves], axis=0)
+        jnp.concatenate([jnp.where(even, half[0:own_rows], half[own_rows : 2 * own_rows]) for half in halves], axis=0),
+        slice(None),
     )
     for k in range(1, NZ):
         source = (z + k) % NZ
         remote(tsend.at[source], trecv.at[source], t_send.at[k], t_recv.at[source], z_peer(source)).wait_recv()
         value = value + trecv[source].astype(jnp.float32)
-    value = value / counts
+    permuted[...] = value / counts
+    place = lax.broadcasted_iota(jnp.int32, (CORES * own_rows, LANES), 1) // GROUP
+    for row_x in range(4):
+        for core in range(CORES):
+            piece_of = None
+            for row_y in range(4):
+                first, second = c * row_x + (1 - c) * row_y, c * row_y + (1 - c) * row_x
+                block = pl.ds(pl.multiple_of((first * 2 + second // 2) * LANES, LANES), LANES)
+                shift = (row_y * GROUP + LANES - (second % 2 * 2 + core) * GROUP) % LANES
+                moved = pltpu.roll(permuted[:, block], shift, 1)
+                piece_of = moved if piece_of is None else jnp.where(place == row_y, moved, piece_of)
+            block = (row_x * CORES + core) * LANES
+            ordered[:, block : block + LANES] = piece_of
+    value = ordered[...]
 
     low, high = value[0:own_rows, :], value[own_rows : 2 * own_rows, :]
     fsend[...] = jnp.where(c == 0, high, low)
@@ -391,11 +454,11 @@
             vmem((NFRAMES, NFRAMES), f32),
             vmem((8, NFRAMES), f32),
             vmem((NFRAMES, 8), f32),
-            vmem((4, CLASS_ROWS, NFRAMES), bf16),
-            vmem((4, CLASS_ROWS, NFRAMES), bf16),
-            vmem((CLASS_ROWS, NFRAMES), f32),
-            vmem((4, SUB_ROWS, NFRAMES), bf16),
-            vmem((4, SUB_ROWS, NFRAMES), bf16),
+            vmem((4, CLASS_ROWS, HELD), bf16),
+            vmem((4, CLASS_ROWS, HELD), bf16),
+            vmem((CLASS_ROWS, HELD), f32),
+            vmem((4, SUB_ROWS, HELD), bf16),
+            vmem((4, SUB_ROWS, HELD), bf16),
             vmem((SUB_ROWS, NFRAMES), f32),
             vmem((NZ, CORES * own_rows, NFRAMES), bf16),
             vmem((NZ, CORES * own_rows, NFRAMES), bf16),
@@ -408,6 +471,10 @@
             vmem((NFRAMES, 8), f32),
             vmem((own_rows, NFRAMES), f32),
             vmem((own_rows, NFRAMES), f32),
+            vmem((4, SUB_ROWS, 2 * LANES), bf16), vmem((4, SUB_ROWS, 2 * LANES), bf16),
+            vmem((4, SUB_ROWS, LANES), bf16), vmem((4, SUB_ROWS, LANES), bf16),
+            vmem((CORES * own_rows, NFRAMES), f32),
+            vmem((CORES * own_rows, NFRAMES), f32),
             dma((4,)),
             dma((CHUNKS,)),
             dma((CHUNKS, NDEV_FRAME)), dma((CHUNKS, NDEV_FRAME)),
@@ -419,6 +486,8 @@
             dma((4,)), dma((4,)),
             dma((NZ,)), dma((NZ,)),
             dma, dma,
+            dma((4,)), dma((4,)),
+            dma((4,)), dma((4,)),
         ],
         compiler_params=pltpu.CompilerParams(
             collective_id=0, has_side_effects=True, vmem_limit_bytes=60 * 2**20

time: 55.8 us -> 56 us (level)
  no operation moved by 1% of the time
where the time goes in v5:
time: 56 us; the launch traced here: 55.8 us
  Pallas kernels  54.4 us (97%)
  local copies, waits for them, and re-layouts  1.4 us (2%)
    pallas_call x1, Pallas kernels, shards(): pl.pallas_call(kernel, out_shape=jax.ShapeDtypeStruct((CYCLES, own_rows,...  54.4 us
    transpose x1, local copies, waits for them, and re-layouts, shards(): return jnp.transpose(out, (1, 0, 2))  1.4 us

profile of v5, /device:TPU:1, one launch (start us, length us, event | category | flops | bytes accessed | tf_op | source)
XLA Modules:
  0.0 55.8 jit_solution(50615058757610792)
XLA Ops:
  0.0 54.4 %shard_map.55 = f32[2,4,1024]{2,1,0:T(4,128)} custom-call(bf16[128,4096]{1,0:T(8,128)(2,1)} %frames.1, f32[32,128]{1,0:T(8,128)} %bitcast.6, s32[32,128]{1,0:T(8,128)} %bitcast.7, s32[32,128]{1,0:T(8,128)} %bitcast.8, s32[32,128]{1,0:T(8,128)} %bitcast.9), custom_call_target="tpu_custom_call" | custom-call | tf_op jit(solution)/shard_map/pallas_call | solution.py:440
  54.4 1.4 %copy.6 = f32[4,2,1024]{2,1,0:T(2,128)} copy(f32[4,2,1024]{2,0,1:T(4,128)} %bitcast.5) | data formatting | bytes 65536 | tf_op jit(solution)/shard_map/transpose | solution.py:496

commit v6 on v5

--- a/solution.py
+++ b/solution.py
@@ -45,7 +45,7 @@
     frames, dead_hbm, band_hbm, label_hbm, valid_hbm,
     out,
     dead, band, label, valid, arrived, rate, smooth, outgoing,
-    gram, sums_ref, sums_t, gsend, grecv, gown, hsend, hrecv, hown, tsend, trecv,
+    gram, sums_ref, sums_t, gsend, grecv, gown, hsend, hrecv, hown, tsend, trecv, usend, urecv,
     stat1, stat2, stat3, statg2, statg3, spread, spread_t,
     fsend, frecv, m1_out, m1_in, m2_out, m2_in, permuted, ordered,
     par_sem, own_sem, a2a_send, a2a_recv, sib_send, sib_recv,
@@ -256,9 +256,11 @@
                 else:
                     gown[rows, n * LANES : (n + 1) * LANES] = centred
 
-    for j in (1, 2, 3, 0):
+    own_side = a2 // 2
+    subs = [(1 - own_side) * 2, (1 - own_side) * 2 + 1, a2 + 1 - a2 % 2 * 2, a2]
+    for sub in subs:
         for k in (2, 1, 3):
-            launch(g_copy(k, (a2 + j) % 4))
+            launch(g_copy(k, sub))
     for k in range(1, 4):
         source = (a1 + k) % 4
         remote(stat1.at[source], stat1.at[source], s1_send.at[k], s1_recv.at[source], first_peer(source)).wait_recv()
@@ -298,12 +300,27 @@
             spread_t[pl.ds(own_start + half * LANES, LANES), :], lane(2, other_half(a1, half))
         )
 
-    def h_copy(k):
-        to = (a2 + k) % 4
-        return remote(hsend.at[to], hrecv.at[a2], h_send.at[k], h_recv.at[a2], second_peer(to))
-
-    for j in (1, 2, 3, 0):
-        sub = (a2 + j) % 4
+    def h_copy(sub):
+        return remote(hsend.at[sub], hrecv.at[a2], h_send.at[sub], h_recv.at[a2], second_peer(sub))
+
+    def mirror(phase, half):
+        rows = pl.ds(pl.multiple_of(half * LANES, LANES), LANES)
+        turned = jnp.transpose(gown[rows, 2 * LANES : 4 * LANES]).astype(jnp.bfloat16)
+        for n in range(4):
+            m1_out[phase, n] = turned[n * SUB_ROWS : (n + 1) * SUB_ROWS, :]
+            launch(
+                remote(
+                    m1_out.at[phase, n], m1_in.at[half, a2], m1_send.at[phase, n], m1_recv.at[half, a2],
+                    peer((a1 + 1) % 4, n),
+                )
+            )
+        turned = jnp.transpose(gown[rows, 4 * LANES :]).astype(jnp.bfloat16)
+        for n in range(2):
+            to = other_half(a1, half) * 2 + n
+            m2_out[to] = turned[n * SUB_ROWS : (n + 1) * SUB_ROWS, :]
+            launch(remote(m2_out.at[to], m2_in.at[a2], m2_send.at[to], m2_recv.at[a2], peer((a1 + 2) % 4, to)))
+
+    for n, sub in enumerate(subs):
         rows = pl.ds(pl.multiple_of(sub * SUB_ROWS, SUB_ROWS), SUB_ROWS)
         for k in range(1, 4):
             source = (a1 + k) % 4
@@ -315,30 +332,13 @@
         for k in range(1, 4):
             value = value + grecv[(a1 + k) % 4, rows, :].astype(jnp.float32)
         gown[rows, :] = value
-        if j:
+        if n < 3:
             hsend[sub] = value.astype(jnp.bfloat16)
-            launch(h_copy(j))
-
-    def mirror_copy(n):
-        return remote(
-            m1_out.at[n], m1_in.at[a2], m1_send.at[n], m1_recv.at[a2], peer((a1 + 1) % 4, n)
-        )
-
-    def half_copy(n):
-        return remote(
-            m2_out.at[n], m2_in.at[a2], m2_send.at[n], m2_recv.at[a2], peer((a1 + 2) % 4, n)
-        )
-
-    mirror = jnp.transpose(gown[:, 2 * LANES : 4 * LANES]).astype(jnp.bfloat16)
-    for n in range(4):
-        m1_out[n] = mirror[n * SUB_ROWS : (n + 1) * SUB_ROWS, :]
-        launch(mirror_copy(n))
-    for half in range(2):
-        mirror = jnp.transpose(gown[half * LANES : (half + 1) * LANES, 4 * LANES :]).astype(jnp.bfloat16)
-        for n in range(2):
-            m2_out[other_half(a1, half) * 2 + n] = mirror[n * SUB_ROWS : (n + 1) * SUB_ROWS, :]
-    for n in range(4):
-        launch(half_copy(n))
+            launch(h_copy(sub))
+        if n == 1:
+            mirror(0, 1 - own_side)
+        if n == 3:
+            mirror(1, own_side)
 
     for k in range(1, 4):
         source = (a2 + k) % 4
@@ -349,44 +349,58 @@
         launch(stat3_copy(k))
     between(stat2, 4)
     row_start = pl.multiple_of(a1 * CLASS_ROWS + a2 * SUB_ROWS, SUB_ROWS)
-    hown[...] = outer(spread_t[pl.ds(row_start, SUB_ROWS), :], slice(None))
+    own_half = other_half(a1, own_side)
+    order = [lane(0, 0), lane(0, 1), lane(1, 0), lane(1, 1), lane(2, own_half)]
+    order += [lane(2, 1 - own_half), lane(3, 0), lane(3, 1)]
+    for n, cols in enumerate(order):
+        hown[:, n * LANES : (n + 1) * LANES] = outer(spread_t[pl.ds(row_start, SUB_ROWS), :], cols)
+    own_rows = GROUP // NZ
+
+    def along_z(part, lanes, buffer, landed, send_sem, recv_sem):
+        for other_z in range(NZ):
+            rows = [
+                hown[core * GROUP + other_z * own_rows : core * GROUP + (other_z + 1) * own_rows, lanes]
+                for core in range(CORES)
+            ]
+            buffer[other_z] = jnp.concatenate(rows, axis=0).astype(jnp.bfloat16)
+        for k in range(1, NZ):
+            to = (z + k) % NZ
+            launch(
+                remote(buffer.at[to], landed.at[z], send_sem.at[part, k], recv_sem.at[part, z], z_peer(to))
+            )
+
+    def from_z(part, buffer, landed, send_sem, recv_sem):
+        value = buffer[z].astype(jnp.float32)
+        for k in range(1, NZ):
+            source = (z + k) % NZ
+            remote(
+                buffer.at[source], landed.at[source], send_sem.at[part, k], recv_sem.at[part, source], z_peer(source)
+            ).wait_recv()
+            value = value + landed[source].astype(jnp.float32)
+        return value
+
     for k in range(1, 4):
         source = (a2 + k) % 4
-        remote(hsend.at[source], hrecv.at[source], h_send.at[k], h_recv.at[source], second_peer(source)).wait_recv()
+        remote(
+            hsend.at[source], hrecv.at[source], h_send.at[source], h_recv.at[source], second_peer(source)
+        ).wait_recv()
     value = gown[pl.ds(pl.multiple_of(a2 * SUB_ROWS, SUB_ROWS), SUB_ROWS), :]
     for k in range(1, 4):
         value = value + hrecv[(a2 + k) % 4].astype(jnp.float32)
-    own_half = other_half(a1, a2 // 2)
-    for n, cols in enumerate((lane(0, 0), lane(0, 1), lane(1, 0), lane(1, 1), lane(2, own_half))):
-        hown[:, cols] += value[:, n * LANES : (n + 1) * LANES]
-    for n in range(4):
-        remote(m1_out.at[n], m1_in.at[n], m1_send.at[n], m1_recv.at[n], peer((a1 + 3) % 4, n)).wait_recv()
-    value = m1_in[0].astype(jnp.float32)
-    for n in range(1, 4):
-        value = value + m1_in[n].astype(jnp.float32)
-    hown[:, lane(3, 0)] += value[:, 0:LANES]
-    hown[:, lane(3, 1)] += value[:, LANES:]
+    hown[:, 0:HELD] += value
+    along_z(0, slice(0, HELD), tsend, trecv, t_send, t_recv)
+
     for n in range(4):
         remote(m2_out.at[n], m2_in.at[n], m2_send.at[n], m2_recv.at[n], peer((a1 + 2) % 4, n)).wait_recv()
-    value = m2_in[0].astype(jnp.float32)
-    for n in range(1, 4):
-        value = value + m2_in[n].astype(jnp.float32)
-    hown[:, lane(2, 1 - own_half)] += value
-    own_rows = GROUP // NZ
-
-    for other_z in range(NZ):
-        rows = jnp.concatenate(
-            [hown[core * GROUP + other_z * own_rows : core * GROUP + (other_z + 1) * own_rows, :] for core in range(CORES)],
-            axis=0,
-        )
-        tsend[other_z] = rows.astype(jnp.bfloat16)
-
-    def t_copy(k):
-        to = (z + k) % NZ
-        return remote(tsend.at[to], trecv.at[z], t_send.at[k], t_recv.at[z], z_peer(to))
-
-    for k in range(1, NZ):
-        launch(t_copy(k))
+        hown[:, HELD : HELD + LANES] += m2_in[n].astype(jnp.float32)
+    for half in range(2):
+        for n in range(4):
+            remote(
+                m1_out.at[half, n], m1_in.at[half, n], m1_send.at[half, n], m1_recv.at[half, n], peer((a1 + 3) % 4, n)
+            ).wait_recv()
+            hown[:, HELD + (half + 1) * LANES : HELD + (half + 2) * LANES] += m1_in[half, n].astype(jnp.float32)
+    along_z(1, slice(HELD, NFRAMES), usend, urecv, t_send, t_recv)
+
     for k in range(1, NZ):
         source = (z + k) % NZ
         remote(statg3, stat3.at[source], s3_send.at[k], s3_recv.at[source], z_peer(source)).wait_recv()
@@ -395,15 +409,17 @@
         spread_t[pl.ds(pl.multiple_of(row_start + core * GROUP + z // 2 * 8, 8), 8), :] for core in range(CORES)
     ]
     even = z % 2 == 0
-    value = tsend[z].astype(jnp.float32) + outer(
+    permuted[...] = outer(
         jnp.concatenate([jnp.where(even, half[0:own_rows], half[own_rows : 2 * own_rows]) for half in halves], axis=0),
         slice(None),
     )
-    for k in range(1, NZ):
-        source = (z + k) % NZ
-        remote(tsend.at[source], trecv.at[source], t_send.at[k], t_recv.at[source], z_peer(source)).wait_recv()
-        value = value + trecv[source].astype(jnp.float32)
-    permuted[...] = value / counts
+    value = from_z(0, tsend, trecv, t_send, t_recv)
+    for n in range(5):
+        permuted[:, order[n]] += value[:, n * LANES : (n + 1) * LANES]
+    value = from_z(1, usend, urecv, t_send, t_recv)
+    for n in range(5, 8):
+        permuted[:, order[n]] += value[:, (n - 5) * LANES : (n - 4) * LANES]
+    permuted[...] = permuted[...] / counts
     place = lax.broadcasted_iota(jnp.int32, (CORES * own_rows, LANES), 1) // GROUP
     for row_x in range(4):
         for core in range(CORES):
@@ -460,8 +476,10 @@
             vmem((4, SUB_ROWS, HELD), bf16),
             vmem((4, SUB_ROWS, HELD), bf16),
             vmem((SUB_ROWS, NFRAMES), f32),
-            vmem((NZ, CORES * own_rows, NFRAMES), bf16),
-            vmem((NZ, CORES * own_rows, NFRAMES), bf16),
+            vmem((NZ, CORES * own_rows, HELD), bf16),
+            vmem((NZ, CORES * own_rows, HELD), bf16),
+            vmem((NZ, CORES * own_rows, NFRAMES - HELD), bf16),
+            vmem((NZ, CORES * own_rows, NFRAMES - HELD), bf16),
             vmem((4, 2, NFRAMES), f32),
             vmem((4, 2, NFRAMES), f32),
             vmem((NZ, 2, NFRAMES), f32),
@@ -471,7 +489,7 @@
             vmem((NFRAMES, 8), f32),
             vmem((own_rows, NFRAMES), f32),
             vmem((own_rows, NFRAMES), f32),
-            vmem((4, SUB_ROWS, 2 * LANES), bf16), vmem((4, SUB_ROWS, 2 * LANES), bf16),
+            vmem((2, 4, SUB_ROWS, LANES), bf16), vmem((2, 4, SUB_ROWS, LANES), bf16),
             vmem((4, SUB_ROWS, LANES), bf16), vmem((4, SUB_ROWS, LANES), bf16),
             vmem((CORES * own_rows, NFRAMES), f32),
             vmem((CORES * own_rows, NFRAMES), f32),
@@ -484,9 +502,9 @@
             dma((NZ,)), dma((NZ,)),
             dma((4, 4)), dma((4, 4)),
             dma((4,)), dma((4,)),
-            dma((NZ,)), dma((NZ,)),
+            dma((2, NZ)), dma((2, NZ)),
             dma, dma,
-            dma((4,)), dma((4,)),
+            dma((2, 4)), dma((2, 4)),
             dma((4,)), dma((4,)),
         ],
         compiler_params=pltpu.CompilerParams(

time: 56 us -> 57 us (1.018)
  Pallas kernels: 54.4 us -> 55.4 us
    pallas_call x1, Pallas kernels: 54.4 us -> 55.4 us  [shards(): pl.pallas_call(kernel, out_shape=jax.ShapeDtypeStruct((CYCLES, own_rows,...]
where the time goes in v6:
time: 57 us; the launch traced here: 56.8 us
  Pallas kernels  55.4 us (97%)
  local copies, waits for them, and re-layouts  1.4 us (2%)
    pallas_call x1, Pallas kernels, shards(): pl.pallas_call(kernel, out_shape=jax.ShapeDtypeStruct((CYCLES, own_rows,...  55.4 us
    transpose x1, local copies, waits for them, and re-layouts, shards(): return jnp.transpose(out, (1, 0, 2))  1.4 us

profile of v6, /device:TPU:1, one launch (start us, length us, event | category | flops | bytes accessed | tf_op | source)
XLA Modules:
  0.0 56.8 jit_solution(8063139474704337594)
XLA Ops:
  0.0 55.4 %shard_map.55 = f32[2,4,1024]{2,1,0:T(4,128)} custom-call(bf16[128,4096]{1,0:T(8,128)(2,1)} %frames.1, f32[32,128]{1,0:T(8,128)} %bitcast.6, s32[32,128]{1,0:T(8,128)} %bitcast.7, s32[32,128]{1,0:T(8,128)} %bitcast.8, s32[32,128]{1,0:T(8,128)} %bitcast.9), custom_call_target="tpu_custom_call" | custom-call | tf_op jit(solution)/shard_map/pallas_call | solution.py:456
  55.4 1.4 %copy.6 = f32[4,2,1024]{2,1,0:T(2,128)} copy(f32[4,2,1024]{2,0,1:T(4,128)} %bitcast.5) | data formatting | bytes 65536 | tf_op jit(solution)/shard_map/transpose | solution.py:514

commit v7 on v5

--- a/solution.py
+++ b/solution.py
@@ -94,10 +94,7 @@
         pl.semaphore_signal(barrier, inc=1, device_id=(f, ((y + k) % NY) * NZ + z), device_id_type=MESH)
     for k in range(1, NZ):
         pl.semaphore_signal(barrier, inc=1, device_id=z_peer((z + k) % NZ), device_id_type=MESH)
-    for k in range(1, 4):
-        for n in range(1, 4):
-            pl.semaphore_signal(barrier, inc=1, device_id=peer((a1 + k) % 4, (a2 + n) % 4), device_id_type=MESH)
-    pl.semaphore_wait(barrier, NDEV_FRAME - 1 + NY - 1 + NZ - 1 + 9)
+    pl.semaphore_wait(barrier, NDEV_FRAME - 1 + NY - 1 + NZ - 1)
 
     def piece(owner, chunk):
         return frames.at[:, pl.ds(pl.multiple_of(owner * OWN_PIX + chunk * LANES, LANES), LANES)]
@@ -112,7 +109,7 @@
         return pltpu.make_async_copy(piece(f, chunk), arrived.at[chunk, f], own_sem.at[chunk])
 
     for chunk in range(CHUNKS):
-        for k in range(1, NDEV_FRAME):
+        for k in (4, 3, 5, 2, 6, 7, 1):
             launch(a2a_copy(k, chunk))
         own_copy(chunk).start()
     params = [
@@ -305,6 +302,14 @@
     for j in (1, 2, 3, 0):
         sub = (a2 + j) % 4
         rows = pl.ds(pl.multiple_of(sub * SUB_ROWS, SUB_ROWS), SUB_ROWS)
+        if j == 0:
+            for k in range(1, 4):
+                source = (a2 + k) % 4
+                remote(statg2, stat2.at[source], s2_send.at[k], s2_recv.at[source], second_peer(source)).wait_recv()
+            statg3[...] = stat2[0] + stat2[1] + stat2[2] + stat2[3]
+            stat3[z] = statg3[...]
+            for k in (4, 3, 5, 2, 6, 1, 7):
+                launch(stat3_copy(k))
         for k in range(1, 4):
             source = (a1 + k) % 4
             remote(
@@ -329,10 +334,6 @@
             m2_out.at[n], m2_in.at[a2], m2_send.at[n], m2_recv.at[a2], peer((a1 + 2) % 4, n)
         )
 
-    mirror = jnp.transpose(gown[:, 2 * LANES : 4 * LANES]).astype(jnp.bfloat16)
-    for n in range(4):
-        m1_out[n] = mirror[n * SUB_ROWS : (n + 1) * SUB_ROWS, :]
-        launch(mirror_copy(n))
     for half in range(2):
         mirror = jnp.transpose(gown[half * LANES : (half + 1) * LANES, 4 * LANES :]).astype(jnp.bfloat16)
         for n in range(2):
@@ -340,16 +341,17 @@
     for n in range(4):
         launch(half_copy(n))
 
-    for k in range(1, 4):
-        source = (a2 + k) % 4
-        remote(statg2, stat2.at[source], s2_send.at[k], s2_recv.at[source], second_peer(source)).wait_recv()
-    statg3[...] = stat2[0] + stat2[1] + stat2[2] + stat2[3]
-    stat3[z] = statg3[...]
-    for k in range(1, NZ):
-        launch(stat3_copy(k))
+    mirror = jnp.transpose(gown[:, 2 * LANES : 4 * LANES]).astype(jnp.bfloat16)
+    for n in range(4):
+        m1_out[n] = mirror[n * SUB_ROWS : (n + 1) * SUB_ROWS, :]
+        launch(mirror_copy(n))
     between(stat2, 4)
     row_start = pl.multiple_of(a1 * CLASS_ROWS + a2 * SUB_ROWS, SUB_ROWS)
-    hown[...] = outer(spread_t[pl.ds(row_start, SUB_ROWS), :], slice(None))
+    column = spread_t[pl.ds(row_start, SUB_ROWS), :]
+    value = column[:, 0:1] * spread[0:1, :]
+    for k in range(1, 4):
+        value = value + column[:, k : k + 1] * spread[k : k + 1, :]
+    hown[...] = value
     for k in range(1, 4):
         source = (a2 + k) % 4
         remote(hsend.at[source], hrecv.at[source], h_send.at[k], h_recv.at[source], second_peer(source)).wait_recv()
@@ -385,7 +387,7 @@
         to = (z + k) % NZ
         return remote(tsend.at[to], trecv.at[z], t_send.at[k], t_recv.at[z], z_peer(to))
 
-    for k in range(1, NZ):
+    for k in (4, 3, 5, 2, 6, 1, 7):
         launch(t_copy(k))
     for k in range(1, NZ):
         source = (z + k) % NZ

time: 56 us -> 54.4 us (0.971)
  Pallas kernels: 54.4 us -> 52.8 us
    pallas_call x1, Pallas kernels: 54.4 us -> 52.8 us  [shards(): pl.pallas_call(kernel, out_shape=jax.ShapeDtypeStruct((CYCLES, own_rows,...]
where the time goes in v7:
time: 54.4 us; the launch traced here: 54.2 us
  Pallas kernels  52.8 us (97%)
  local copies, waits for them, and re-layouts  1.4 us (3%)
    pallas_call x1, Pallas kernels, shards(): pl.pallas_call(kernel, out_shape=jax.ShapeDtypeStruct((CYCLES, own_rows,...  52.8 us
    transpose x1, local copies, waits for them, and re-layouts, shards(): return jnp.transpose(out, (1, 0, 2))  1.4 us

profile of v7, /device:TPU:1, one launch (start us, length us, event | category | flops | bytes accessed | tf_op | source)
XLA Modules:
  0.0 54.2 jit_solution(16188345402770796095)
XLA Ops:
  0.0 52.8 %shard_map.55 = f32[2,4,1024]{2,1,0:T(4,128)} custom-call(bf16[128,4096]{1,0:T(8,128)(2,1)} %frames.1, f32[32,128]{1,0:T(8,128)} %bitcast.6, s32[32,128]{1,0:T(8,128)} %bitcast.7, s32[32,128]{1,0:T(8,128)} %bitcast.8, s32[32,128]{1,0:T(8,128)} %bitcast.9), custom_call_target="tpu_custom_call" | custom-call | tf_op jit(solution)/shard_map/pallas_call | solution.py:442
  52.8 1.4 %copy.6 = f32[4,2,1024]{2,1,0:T(2,128)} copy(f32[4,2,1024]{2,0,1:T(4,128)} %bitcast.5) | data formatting | bytes 65536 | tf_op jit(solution)/shard_map/transpose | solution.py:498

commit v8 on v7

--- a/solution.py
+++ b/solution.py
@@ -47,7 +47,7 @@
     dead, band, label, valid, arrived, rate, smooth, outgoing,
     gram, sums_ref, sums_t, gsend, grecv, gown, hsend, hrecv, hown, tsend, trecv,
     stat1, stat2, stat3, statg2, statg3, spread, spread_t,
-    fsend, frecv, m1_out, m1_in, m2_out, m2_in, permuted, ordered,
+    fsend, frecv, m1_out, m1_in, m2_out, m2_in, permuted,
     par_sem, own_sem, a2a_send, a2a_recv, sib_send, sib_recv,
     s1_send, s1_recv, s2_send, s2_recv, s3_send, s3_recv,
     g_send, g_recv, h_send, h_recv, t_send, t_recv, f_send, f_recv,
@@ -178,7 +178,7 @@
                 )
             return 0
 
-        lax.fori_loop(0, NDEV_FRAME, correct, 0)
+        lax.fori_loop(0, NDEV_FRAME, correct, 0, unroll=2)
 
         def window(start):
             total = rate[pl.ds(start + PAD, GROUP), :]
@@ -204,7 +204,7 @@
             frame = start + lax.broadcasted_iota(jnp.int32, (GROUP, LANES), 0)
             span = jnp.minimum(frame + width, NFRAMES - 1) - jnp.maximum(frame - width, 0) + 1
             put(start // GROUP, window(start) / span.astype(jnp.float32))
-        lax.fori_loop(1, NFRAMES // GROUP - 1, inside, 0)
+        lax.fori_loop(1, NFRAMES // GROUP - 1, inside, 0, unroll=3)
         launch(sib_copy(chunk))
         if chunk:
             accumulate(chunk - 1)
@@ -377,18 +377,21 @@
     own_rows = GROUP // NZ
 
     for other_z in range(NZ):
-        rows = jnp.concatenate(
-            [hown[core * GROUP + other_z * own_rows : core * GROUP + (other_z + 1) * own_rows, :] for core in range(CORES)],
-            axis=0,
-        )
-        tsend[other_z] = rows.astype(jnp.bfloat16)
-
-    def t_copy(k):
-        to = (z + k) % NZ
-        return remote(tsend.at[to], trecv.at[z], t_send.at[k], t_recv.at[z], z_peer(to))
+        for core in range(CORES):
+            start = core * GROUP + other_z * own_rows
+            tsend[other_z, core] = hown[start : start + own_rows, :].astype(jnp.bfloat16)
+
+    def t_copy(k, flip):
+        to, core = (z + k) % NZ, (c + flip) % CORES
+        return remote(
+            tsend.at[to, core], trecv.at[c, z], t_send.at[k, flip], t_recv.at[c, z], (x * CORES + core, y * NZ + to)
+        )
 
     for k in (4, 3, 5, 2, 6, 1, 7):
-        launch(t_copy(k))
+        for flip in range(CORES):
+            launch(t_copy(k, flip))
+    launch(t_copy(0, 1))
+    trecv[c, z] = tsend[z, c]
     for k in range(1, NZ):
         source = (z + k) % NZ
         remote(statg3, stat3.at[source], s3_send.at[k], s3_recv.at[source], z_peer(source)).wait_recv()
@@ -397,36 +400,44 @@
         spread_t[pl.ds(pl.multiple_of(row_start + core * GROUP + z // 2 * 8, 8), 8), :] for core in range(CORES)
     ]
     even = z % 2 == 0
-    value = tsend[z].astype(jnp.float32) + outer(
+    term = outer(
         jnp.concatenate([jnp.where(even, half[0:own_rows], half[own_rows : 2 * own_rows]) for half in halves], axis=0),
         slice(None),
     )
-    for k in range(1, NZ):
-        source = (z + k) % NZ
-        remote(tsend.at[source], trecv.at[source], t_send.at[k], t_recv.at[source], z_peer(source)).wait_recv()
-        value = value + trecv[source].astype(jnp.float32)
-    permuted[...] = value / counts
-    place = lax.broadcasted_iota(jnp.int32, (CORES * own_rows, LANES), 1) // GROUP
-    for row_x in range(4):
-        for core in range(CORES):
-            piece_of = None
-            for row_y in range(4):
-                first, second = c * row_x + (1 - c) * row_y, c * row_y + (1 - c) * row_x
-                block = pl.ds(pl.multiple_of((first * 2 + second // 2) * LANES, LANES), LANES)
-                shift = (row_y * GROUP + LANES - (second % 2 * 2 + core) * GROUP) % LANES
-                moved = pltpu.roll(permuted[:, block], shift, 1)
-                piece_of = moved if piece_of is None else jnp.where(place == row_y, moved, piece_of)
-            block = (row_x * CORES + core) * LANES
-            ordered[:, block : block + LANES] = piece_of
-    value = ordered[...]
-
-    low, high = value[0:own_rows, :], value[own_rows : 2 * own_rows, :]
-    fsend[...] = jnp.where(c == 0, high, low)
+    low, high = term[0:own_rows, :], term[own_rows : 2 * own_rows, :]
+    fsend[...] = jnp.broadcast_to(counts, (2 * own_rows, NFRAMES))
+    fsend[0:own_rows, :] = jnp.where(c == 0, high, low)
     last = remote(fsend, frecv, f_send, f_recv, sibling)
     launch(last)
-    out[c] = jnp.where(c == 0, low, high)
+
+    place = lax.broadcasted_iota(jnp.int32, (own_rows, LANES), 1) // GROUP
+
+    def give(cycle, flip, value, count):
+        for k in range(NZ):
+            source, core = (z + k) % NZ, (c + flip) % CORES
+            if k or flip:
+                remote(
+                    tsend.at[source, core], trecv.at[cycle, source], t_send.at[k, flip], t_recv.at[cycle, source],
+                    (x * CORES + core, y * NZ + source),
+                ).wait_recv()
+            value = value + trecv[cycle, source].astype(jnp.float32)
+        permuted[flip] = value / count
+        for row_x in range(4):
+            for core in range(CORES):
+                piece_of = None
+                for row_y in range(4):
+                    first = cycle * row_x + (1 - cycle) * row_y
+                    second = cycle * row_y + (1 - cycle) * row_x
+                    block = pl.ds(pl.multiple_of((first * 2 + second // 2) * LANES, LANES), LANES)
+                    shift = (row_y * GROUP + LANES - (second % 2 * 2 + core) * GROUP) % LANES
+                    moved = pltpu.roll(permuted[flip, :, block], shift, 1)
+                    piece_of = moved if piece_of is None else jnp.where(place == row_y, moved, piece_of)
+                block = (row_x * CORES + core) * LANES
+                out[cycle, :, block : block + LANES] = piece_of
+
+    give(c, 0, jnp.where(c == 0, low, high), counts)
     last.wait_recv()
-    out[1 - c] = frecv[...]
+    give(1 - c, 1, frecv[0:own_rows, :], frecv[own_rows : own_rows + 1, :])
 
     finish()
 
@@ -462,8 +473,8 @@
             vmem((4, SUB_ROWS, HELD), bf16),
             vmem((4, SUB_ROWS, HELD), bf16),
             vmem((SUB_ROWS, NFRAMES), f32),
-            vmem((NZ, CORES * own_rows, NFRAMES), bf16),
-            vmem((NZ, CORES * own_rows, NFRAMES), bf16),
+            vmem((NZ, CORES, own_rows, NFRAMES), bf16),
+            vmem((CORES, NZ, own_rows, NFRAMES), bf16),
             vmem((4, 2, NFRAMES), f32),
             vmem((4, 2, NFRAMES), f32),
             vmem((NZ, 2, NFRAMES), f32),
@@ -471,12 +482,11 @@
             vmem((2, NFRAMES), f32),
             vmem((8, NFRAMES), f32),
             vmem((NFRAMES, 8), f32),
-            vmem((own_rows, NFRAMES), f32),
-            vmem((own_rows, NFRAMES), f32),
+            vmem((2 * own_rows, NFRAMES), f32),
+            vmem((2 * own_rows, NFRAMES), f32),
             vmem((4, SUB_ROWS, 2 * LANES), bf16), vmem((4, SUB_ROWS, 2 * LANES), bf16),
             vmem((4, SUB_ROWS, LANES), bf16), vmem((4, SUB_ROWS, LANES), bf16),
-            vmem((CORES * own_rows, NFRAMES), f32),
-            vmem((CORES * own_rows, NFRAMES), f32),
+            vmem((CORES, own_rows, NFRAMES), f32),
             dma((4,)),
             dma((CHUNKS,)),
             dma((CHUNKS, NDEV_FRAME)), dma((CHUNKS, NDEV_FRAME)),
@@ -486,7 +496,7 @@
             dma((NZ,)), dma((NZ,)),
             dma((4, 4)), dma((4, 4)),
             dma((4,)), dma((4,)),
-            dma((NZ,)), dma((NZ,)),
+            dma((NZ, CORES)), dma((CORES, NZ)),
             dma, dma,
             dma((4,)), dma((4,)),
             dma((4,)), dma((4,)),

time: 54.4 us -> 53 us (0.974)
  Pallas kernels: 52.8 us -> 51.4 us
    pallas_call x1, Pallas kernels: 52.8 us -> 51.4 us  [shards(): pl.pallas_call(kernel, out_shape=jax.ShapeDtypeStruct((CYCLES, own_rows,...]
where the time goes in v8:
time: 53 us; the launch traced here: 52.8 us
  Pallas kernels  51.4 us (97%)
  local copies, waits for them, and re-layouts  1.4 us (3%)
    pallas_call x1, Pallas kernels, shards(): pl.pallas_call(kernel, out_shape=jax.ShapeDtypeStruct((CYCLES, own_rows,...  51.4 us
    transpose x1, local copies, waits for them, and re-layouts, shards(): return jnp.transpose(out, (1, 0, 2))  1.4 us

profile of v8, /device:TPU:1, one launch (start us, length us, event | category | flops | bytes accessed | tf_op | source)
XLA Modules:
  0.0 52.8 jit_solution(16769017072491732487)
XLA Ops:
  0.0 51.4 %shard_map.55 = f32[2,4,1024]{2,1,0:T(4,128)} custom-call(bf16[128,4096]{1,0:T(8,128)(2,1)} %frames.1, f32[32,128]{1,0:T(8,128)} %bitcast.6, s32[32,128]{1,0:T(8,128)} %bitcast.7, s32[32,128]{1,0:T(8,128)} %bitcast.8, s32[32,128]{1,0:T(8,128)} %bitcast.9), custom_call_target="tpu_custom_call" | custom-call | tf_op jit(solution)/shard_map/pallas_call | solution.py:453
  51.4 1.4 %copy.6 = f32[4,2,1024]{2,1,0:T(2,128)} copy(f32[4,2,1024]{2,0,1:T(4,128)} %bitcast.5) | data formatting | bytes 65536 | tf_op jit(solution)/shard_map/transpose | solution.py:508

commit v9 on v8

--- a/solution.py
+++ b/solution.py
@@ -178,7 +178,7 @@
                 )
             return 0
 
-        lax.fori_loop(0, NDEV_FRAME, correct, 0, unroll=2)
+        lax.fori_loop(0, NDEV_FRAME, correct, 0, unroll=4)
 
         def window(start):
             total = rate[pl.ds(start + PAD, GROUP), :]
@@ -204,7 +204,7 @@
             frame = start + lax.broadcasted_iota(jnp.int32, (GROUP, LANES), 0)
             span = jnp.minimum(frame + width, NFRAMES - 1) - jnp.maximum(frame - width, 0) + 1
             put(start // GROUP, window(start) / span.astype(jnp.float32))
-        lax.fori_loop(1, NFRAMES // GROUP - 1, inside, 0, unroll=3)
+        lax.fori_loop(1, NFRAMES // GROUP - 1, inside, 0, unroll=5)
         launch(sib_copy(chunk))
         if chunk:
             accumulate(chunk - 1)
@@ -361,37 +361,7 @@
     own_half = other_half(a1, a2 // 2)
     for n, cols in enumerate((lane(0, 0), lane(0, 1), lane(1, 0), lane(1, 1), lane(2, own_half))):
         hown[:, cols] += value[:, n * LANES : (n + 1) * LANES]
-    for n in range(4):
-        remote(m1_out.at[n], m1_in.at[n], m1_send.at[n], m1_recv.at[n], peer((a1 + 3) % 4, n)).wait_recv()
-    value = m1_in[0].astype(jnp.float32)
-    for n in range(1, 4):
-        value = value + m1_in[n].astype(jnp.float32)
-    hown[:, lane(3, 0)] += value[:, 0:LANES]
-    hown[:, lane(3, 1)] += value[:, LANES:]
-    for n in range(4):
-        remote(m2_out.at[n], m2_in.at[n], m2_send.at[n], m2_recv.at[n], peer((a1 + 2) % 4, n)).wait_recv()
-    value = m2_in[0].astype(jnp.float32)
-    for n in range(1, 4):
-        value = value + m2_in[n].astype(jnp.float32)
-    hown[:, lane(2, 1 - own_half)] += value
     own_rows = GROUP // NZ
-
-    for other_z in range(NZ):
-        for core in range(CORES):
-            start = core * GROUP + other_z * own_rows
-            tsend[other_z, core] = hown[start : start + own_rows, :].astype(jnp.bfloat16)
-
-    def t_copy(k, flip):
-        to, core = (z + k) % NZ, (c + flip) % CORES
-        return remote(
-            tsend.at[to, core], trecv.at[c, z], t_send.at[k, flip], t_recv.at[c, z], (x * CORES + core, y * NZ + to)
-        )
-
-    for k in (4, 3, 5, 2, 6, 1, 7):
-        for flip in range(CORES):
-            launch(t_copy(k, flip))
-    launch(t_copy(0, 1))
-    trecv[c, z] = tsend[z, c]
     for k in range(1, NZ):
         source = (z + k) % NZ
         remote(statg3, stat3.at[source], s3_send.at[k], s3_recv.at[source], z_peer(source)).wait_recv()
@@ -410,6 +380,35 @@
     last = remote(fsend, frecv, f_send, f_recv, sibling)
     launch(last)
 
+    for n in range(4):
+        remote(m1_out.at[n], m1_in.at[n], m1_send.at[n], m1_recv.at[n], peer((a1 + 3) % 4, n)).wait_recv()
+    value = m1_in[0].astype(jnp.float32)
+    for n in range(1, 4):
+        value = value + m1_in[n].astype(jnp.float32)
+    hown[:, lane(3, 0)] += value[:, 0:LANES]
+    hown[:, lane(3, 1)] += value[:, LANES:]
+    for n in range(4):
+        remote(m2_out.at[n], m2_in.at[n], m2_send.at[n], m2_recv.at[n], peer((a1 + 2) % 4, n)).wait_recv()
+    value = m2_in[0].astype(jnp.float32)
+    for n in range(1, 4):
+        value = value + m2_in[n].astype(jnp.float32)
+    hown[:, lane(2, 1 - own_half)] += value
+    for other_z in range(NZ):
+        for core in range(CORES):
+            start = core * GROUP + other_z * own_rows
+            tsend[other_z, core] = hown[start : start + own_rows, :].astype(jnp.bfloat16)
+
+    def t_copy(k, flip):
+        to, core = (z + k) % NZ, (c + flip) % CORES
+        return remote(
+            tsend.at[to, core], trecv.at[c, z], t_send.at[k, flip], t_recv.at[c, z], (x * CORES + core, y * NZ + to)
+        )
+
+    for flip in (1, 0):
+        for k in (4, 3, 5, 2, 6, 1, 7):
+            launch(t_copy(k, flip))
+    launch(t_copy(0, 1))
+    trecv[c, z] = tsend[z, c]
     place = lax.broadcasted_iota(jnp.int32, (own_rows, LANES), 1) // GROUP
 
     def give(cycle, flip, value, count):

time: 53 us -> 52.7 us (level)
  no operation moved by 1% of the time
where the time goes in v9:
time: 52.7 us; the launch traced here: 52.5 us
  Pallas kernels  51.1 us (97%)
  local copies, waits for them, and re-layouts  1.4 us (3%)
    pallas_call x1, Pallas kernels, shards(): pl.pallas_call(kernel, out_shape=jax.ShapeDtypeStruct((CYCLES, own_rows,...  51.1 us
    transpose x1, local copies, waits for them, and re-layouts, shards(): return jnp.transpose(out, (1, 0, 2))  1.4 us

profile of v9, /device:TPU:1, one launch (start us, length us, event | category | flops | bytes accessed | tf_op | source)
XLA Modules:
  0.0 52.5 jit_solution(6443635633206803411)
XLA Ops:
  0.0 51.1 %shard_map.55 = f32[2,4,1024]{2,1,0:T(4,128)} custom-call(bf16[128,4096]{1,0:T(8,128)(2,1)} %frames.1, f32[32,128]{1,0:T(8,128)} %bitcast.6, s32[32,128]{1,0:T(8,128)} %bitcast.7, s32[32,128]{1,0:T(8,128)} %bitcast.8, s32[32,128]{1,0:T(8,128)} %bitcast.9), custom_call_target="tpu_custom_call" | custom-call | tf_op jit(solution)/shard_map/pallas_call | solution.py:452
  51.1 1.4 %copy.6 = f32[4,2,1024]{2,1,0:T(2,128)} copy(f32[4,2,1024]{2,0,1:T(4,128)} %bitcast.5) | data formatting | bytes 65536 | tf_op jit(solution)/shard_map/transpose | solution.py:507

commit v10 on v9

--- a/solution.py
+++ b/solution.py
@@ -337,9 +337,9 @@
     for half in range(2):
         mirror = jnp.transpose(gown[half * LANES : (half + 1) * LANES, 4 * LANES :]).astype(jnp.bfloat16)
         for n in range(2):
-            m2_out[other_half(a1, half) * 2 + n] = mirror[n * SUB_ROWS : (n + 1) * SUB_ROWS, :]
-    for n in range(4):
-        launch(half_copy(n))
+            to = other_half(a1, half) * 2 + n
+            m2_out[to] = mirror[n * SUB_ROWS : (n + 1) * SUB_ROWS, :]
+            launch(half_copy(to))
 
     mirror = jnp.transpose(gown[:, 2 * LANES : 4 * LANES]).astype(jnp.bfloat16)
     for n in range(4):

time: 52.7 us -> 52.8 us (level)
  no operation moved by 1% of the time
where the time goes in v10:
time: 52.8 us; the launch traced here: 52.6 us
  Pallas kernels  51.2 us (97%)
  local copies, waits for them, and re-layouts  1.4 us (3%)
    pallas_call x1, Pallas kernels, shards(): pl.pallas_call(kernel, out_shape=jax.ShapeDtypeStruct((CYCLES, own_rows,...  51.2 us
    transpose x1, local copies, waits for them, and re-layouts, shards(): return jnp.transpose(out, (1, 0, 2))  1.4 us

profile of v10, /device:TPU:1, one launch (start us, length us, event | category | flops | bytes accessed | tf_op | source)
XLA Modules:
  0.0 52.6 jit_solution(13182425042105812001)
XLA Ops:
  0.0 51.2 %shard_map.55 = f32[2,4,1024]{2,1,0:T(4,128)} custom-call(bf16[128,4096]{1,0:T(8,128)(2,1)} %frames.1, f32[32,128]{1,0:T(8,128)} %bitcast.6, s32[32,128]{1,0:T(8,128)} %bitcast.7, s32[32,128]{1,0:T(8,128)} %bitcast.8, s32[32,128]{1,0:T(8,128)} %bitcast.9), custom_call_target="tpu_custom_call" | custom-call | tf_op jit(solution)/shard_map/pallas_call | solution.py:452
  51.2 1.4 %copy.6 = f32[4,2,1024]{2,1,0:T(2,128)} copy(f32[4,2,1024]{2,0,1:T(4,128)} %bitcast.5) | data formatting | bytes 65536 | tf_op jit(solution)/shard_map/transpose | solution.py:507

commit v11 on v8

--- a/solution.py
+++ b/solution.py
@@ -387,8 +387,8 @@
             tsend.at[to, core], trecv.at[c, z], t_send.at[k, flip], t_recv.at[c, z], (x * CORES + core, y * NZ + to)
         )
 
-    for k in (4, 3, 5, 2, 6, 1, 7):
-        for flip in range(CORES):
+    for flip in (1, 0):
+        for k in (4, 3, 5, 2, 6, 1, 7):
             launch(t_copy(k, flip))
     launch(t_copy(0, 1))
     trecv[c, z] = tsend[z, c]

time: 53 us -> 52.8 us (level)
  no operation moved by 1% of the time
where the time goes in v11:
time: 52.8 us; the launch traced here: 52.6 us
  Pallas kernels  51.2 us (97%)
  local copies, waits for them, and re-layouts  1.4 us (3%)
    pallas_call x1, Pallas kernels, shards(): pl.pallas_call(kernel, out_shape=jax.ShapeDtypeStruct((CYCLES, own_rows,...  51.2 us
    transpose x1, local copies, waits for them, and re-layouts, shards(): return jnp.transpose(out, (1, 0, 2))  1.4 us

profile of v11, /device:TPU:1, one launch (start us, length us, event | category | flops | bytes accessed | tf_op | source)
XLA Modules:
  0.0 52.6 jit_solution(3819253319374718461)
XLA Ops:
  0.0 51.2 %shard_map.55 = f32[2,4,1024]{2,1,0:T(4,128)} custom-call(bf16[128,4096]{1,0:T(8,128)(2,1)} %frames.1, f32[32,128]{1,0:T(8,128)} %bitcast.6, s32[32,128]{1,0:T(8,128)} %bitcast.7, s32[32,128]{1,0:T(8,128)} %bitcast.8, s32[32,128]{1,0:T(8,128)} %bitcast.9), custom_call_target="tpu_custom_call" | custom-call | tf_op jit(solution)/shard_map/pallas_call | solution.py:453
  51.2 1.4 %copy.6 = f32[4,2,1024]{2,1,0:T(2,128)} copy(f32[4,2,1024]{2,0,1:T(4,128)} %bitcast.5) | data formatting | bytes 65536 | tf_op jit(solution)/shard_map/transpose | solution.py:508
